TPU v7x, 256 devices: a whole 4x4x8 slice. The times are simulated.
256 devices in a mesh: seg: 8 (over z_hi, core), shard: 16 (over x, y), tok: 2 (over z_lo).
Axes of the slice: x: 4, y: 4, z: 8 (z_hi: 4, z_lo: 2; z = z_hi * 2 + z_lo), core: 2. Of those that a mesh axis runs over, the one named last changes fastest.
Arguments:
- activations: bfloat16 [768, 2560], P('tok', 'shard'), may hold values from -6 to 6
- gate_weight: bfloat16 [2560, 10240], P('shard', 'seg'), may hold values from -0.125 to 0.125
- up_weight: bfloat16 [2560, 10240], P('shard', 'seg'), may hold values from -0.125 to 0.125
- down_weight: bfloat16 [10240, 2560], P('seg', 'shard'), may hold values from -0.0625 to 0.0625
- encoder_weight: bfloat16 [2560, 65536], P(None, ('seg', 'shard')), may hold values from -0.125 to 0.125
- encoder_bias: float32 [65536], P(('seg', 'shard')), may hold values from -0.6 to 0.2
- decoder_weight: bfloat16 [65536, 2560], P(('seg', 'shard')), may hold values from -0.0625 to 0.0625
- decoder_bias: float32 [2560], replicated, may hold values from -1.5 to 1.5
- segment_sizes: int32 [8], replicated, may hold values from 4096 to 8192, as said below
Outputs:
- grad_encoder: float32 [2560, 65536], P('tok', ('seg', 'shard'))
- grad_decoder: float32 [65536, 2560], P(('seg', 'shard'), 'tok')
- prefix_mse: float32 [8], P('seg')
Inputs may be any that keep to these rules, and one draw needn't show every extreme that they name: `segment_sizes`: at least one segment has all 8192 latents live.
All inputs are finite; a program needn't handle non-finite values.
Results may differ from a plain program's by a relative error of at most 0.0078.
Values may be sent and summed in bfloat16 or wider, within the bound.
No kernel may reach another device: no remote copies, remote signals or barrier semaphores. Data moves between devices by JAX's collectives and lax.ppermute only.
A program may use at most 64 MiB of HBM per device.

v0:
```python
import math

import jax
import jax.numpy as jnp
from jax import lax
from jax.sharding import PartitionSpec as P


def carried_in(value, axis, join, neutral, backward):
    count, mine = (lax.axis_size(axis), lax.axis_index(axis))
    pieces = lax.all_gather(value, axis)
    if backward:
        pieces = pieces[::-1]
        mine = count - 1 - mine
    subtotal = jnp.full_like(value, 0) + jnp.asarray(neutral, value.dtype)

    def hop(position, subtotal):
        longer = join(subtotal, pieces[position])
        return jnp.where(position < mine, longer, subtotal)

    return lax.fori_loop(0, count - 1, hop, subtotal)


def local(
    activations,
    gate_weight,
    up_weight,
    down_weight,
    encoder_weight,
    encoder_bias,
    decoder_weight,
    decoder_bias,
    segment_sizes,
):
    shard_index = lax.axis_index("shard")
    segment_index = lax.axis_index("seg")
    tok_rows = activations.shape[0]
    width_slice = activations.shape[1]
    gate_part = jnp.dot(activations, gate_weight, preferred_element_type=jnp.float32)
    up_part = jnp.dot(activations, up_weight, preferred_element_type=jnp.float32)
    gate_total, up_total = lax.psum((gate_part, up_part), "shard")
    hidden = (jax.nn.gelu(gate_total, approximate=True) * up_total).astype(jnp.bfloat16)
    down_part = jnp.dot(hidden, down_weight, preferred_element_type=jnp.float32)
    mlp_slice = lax.psum(down_part, "seg").astype(jnp.bfloat16)
    mlp_full = lax.all_gather(mlp_slice, "shard", axis=1, tiled=True)
    width = mlp_full.shape[1]
    groups = lax.axis_size("tok")
    tokens_all = tok_rows * groups
    mlp_float = mlp_full.astype(jnp.float32)
    centered = (mlp_float - decoder_bias).astype(jnp.bfloat16)
    lat_count = encoder_weight.shape[1]
    segment_total = segment_sizes.shape[0]
    size_here = jnp.sum(jnp.where(jnp.arange(segment_total) == segment_index, segment_sizes, 0))
    latent_index = shard_index * lat_count + jnp.arange(lat_count)
    live_mask = latent_index < size_here
    pre_act = jnp.dot(centered, encoder_weight, preferred_element_type=jnp.float32) + encoder_bias
    latent_codes = jnp.where(live_mask, jax.nn.softplus(10.0 * pre_act) / 10.0, 0.0).astype(
        jnp.bfloat16
    )
    slope = jnp.where(live_mask, jax.nn.sigmoid(10.0 * pre_act), 0.0)
    columns = decoder_weight
    my_part = lax.psum_scatter(
        lax.dot_general(
            columns, latent_codes, (((0,), (1,)), ((), ())), preferred_element_type=jnp.float32
        ),
        "shard",
        scatter_dimension=0,
        tiled=True,
    )
    column_start = shard_index * width_slice
    target = lax.dynamic_slice_in_dim(mlp_float, column_start, width_slice, 1).T
    bias_slice = lax.dynamic_slice_in_dim(decoder_bias, column_start, width_slice, 0)[:, None]
    blank = jnp.zeros_like(my_part)
    earlier = carried_in(my_part, "seg", jnp.add, blank, False)
    errors = bias_slice + (earlier + my_part) - target
    total_square = lax.psum(jnp.sum(errors * errors), ("shard", "tok"))
    prefix_mse = (total_square / (tokens_all * width)).reshape(1)
    later = carried_in(errors, "seg", jnp.add, blank, True)
    back = ((later + errors) * (1.0 / math.sqrt(tokens_all))).astype(jnp.bfloat16)
    piece = lax.all_gather(back, "shard", axis=0, tiled=True)
    columns = decoder_weight
    code_acc = lax.dot_general(
        piece, columns, (((0,), (1,)), ((), ())), preferred_element_type=jnp.float32
    )
    grad_piece = lax.dot_general(
        latent_codes, piece, (((0,), (1,)), ((), ())), preferred_element_type=jnp.float32
    )
    code_grad = (code_acc * slope).astype(jnp.bfloat16)
    encoder_grad = lax.dot_general(
        centered, code_grad, (((0,), (0,)), ((), ())), preferred_element_type=jnp.float32
    )
    grad_encoder = lax.psum_scatter(encoder_grad, "tok", scatter_dimension=0, tiled=True)
    grad_decoder = lax.psum_scatter(grad_piece, "tok", scatter_dimension=1, tiled=True)
    return (grad_encoder, grad_decoder, prefix_mse)


def solution(mesh):
    in_specs = (
        P("tok", "shard"),
        P("shard", "seg"),
        P("shard", "seg"),
        P("seg", "shard"),
        P(None, ("seg", "shard")),
        P(("seg", "shard")),
        P(("seg", "shard"), None),
        P(),
        P(),
    )
    out_specs = (P("tok", ("seg", "shard")), P(("seg", "shard"), "tok"), P("seg"))
    return jax.shard_map(local, mesh=mesh, in_specs=in_specs, out_specs=out_specs, check_vma=False)
```

profile of v0, /device:TPU:1, one launch (start us, length us, event | category | flops | bytes accessed | tf_op | source)
XLA Modules:
  0.0 602.7 jit_solution(8608097557932764812)
XLA Ops:
  7.2 2.9 fusion.35
  10.2 1.7 fusion.36
  12.0 114.8 %all-reduce.4.cloned.1.call-done = (f32[384,1280]{1,0:T(8,128)}, f32[384,1280]{1,0:T(8,128)}) async-done(((f32[384,1280]{1,0:T(8,128)}, f32[384,1280]{1,0:T(8,128)}), (f32[384,1280]{1,0:T(8,128)}, f32[384,1280]{1,0:T(8,128)})) %all-reduce.4.cloned.1.call-update) | async-done | bytes 3932176 | tf_op jit(solution)/shard_map/psum | solution.py:41
  126.8 3.1 fusion.12
  129.8 30.9 %all-reduce.5 = bf16[384,160]{0,1:T(8,128)(2,1)} all-reduce(f32[384,160]{0,1:T(8,128)S(1)} %fusion.12), channel_id=1, replica_groups=mesh['seg'=8,'shard'=16,'tok'=2] {'seg'}, use_global_device_ids=true, to_apply=%region_2.0 | all-reduce | flops 61440 | bytes 368640 | tf_op jit(solution)/shard_map/psum | solution.py:44
  162.1 47.5 %all-gather.7.cloned.1.call-done = bf16[384,2560]{0,1:T(8,128)(2,1)} async-done(((bf16[384,160]{0,1:T(8,128)(2,1)}), bf16[384,2560]{0,1:T(8,128)(2,1)}) %all-gather.7.cloned.1.call-update) | async-done | bytes 1966096 | tf_op jit(solution)/shard_map/all_gather | solution.py:45
  209.6 4.0 fusion.9
  214.5 3.6 convolution_bitcast_fusion
  218.2 82.0 %reduce-scatter.4.cloned.1.call-done = f32[160,384]{1,0:T(8,128)} async-done(((f32[2560,384]{1,0:T(8,128)}), f32[160,384]{1,0:T(8,128)}) %reduce-scatter.4.cloned.1.call-update) | async-done | bytes 245776 | tf_op jit(solution)/shard_map/reduce_scatter | solution.py:62
  300.3 3.7 convert_element_type.23
  304.0 33.6 %all-gather.11.cloned.1.call-done = f32[1280,384]{1,0:T(8,128)} async-done(((f32[160,384]{1,0:T(8,128)}), f32[1280,384]{1,0:T(8,128)}) %all-gather.11.cloned.1.call-update) | async-done | bytes 1966096 | tf_op jit(solution)/shard_map/all_gather | solution.py:11
  337.6 7.2 %while.28 = (s32[]{:T(128)}, f32[160,384]{1,0:T(8,128)S(1)}, s32[]{:T(128)}, f32[8,160,384]{2,1,0:T(8,128)}, s32[]{:T(128)}, /*index=5*/s32[]{:T(128)}) while((s32[]{:T(128)}, f32[160,384]{1,0:T(8,128)S(1)}, s32[]{:T(128)}, f32[8,160,384]{2,1,0:T(8,128)}, s32[]{:T(128)}, /*index=5*/s32[]{:T(128)}) %tuple.87), condition=%wide.region_6.7_spmd.clone, body=%wide.region_5.6_spmd.clone.sunk | while | flops 184324 | bytes 737381 | solution.py:21
  340.7 1.0 add_select_fusion.4
  344.9 2.3 multiply_reduce_fusion
  347.3 33.5 %all-gather.13.cloned.1.call-done = f32[1280,384]{1,0:T(8,128)} async-done(((f32[160,384]{1,0:T(8,128)}), f32[1280,384]{1,0:T(8,128)}) %all-gather.13.cloned.1.call-update) | async-done | bytes 1966096 | tf_op jit(solution)/shard_map/all_gather | solution.py:11
  380.7 3.0 rev.3
  383.7 7.3 %while.29 = (s32[]{:T(128)}, f32[160,384]{1,0:T(8,128)S(1)}, s32[]{:T(128)}, f32[8,160,384]{2,1,0:T(8,128)}, s32[]{:T(128)}, /*index=5*/s32[]{:T(128)}) while((s32[]{:T(128)}, f32[160,384]{1,0:T(8,128)S(1)}, s32[]{:T(128)}, f32[8,160,384]{2,1,0:T(8,128)}, s32[]{:T(128)}, /*index=5*/s32[]{:T(128)}) %tuple.67), condition=%wide.region_8.9_spmd.clone, body=%wide.region_7.8_spmd.clone.sunk | while | flops 184324 | bytes 737381 | solution.py:21
  383.7 1.1 add_select_fusion.5
  391.8 47.0 %all-gather.9.cloned.1.call-done = bf16[2560,384]{1,0:T(8,128)(2,1)} async-done(((bf16[160,384]{1,0:T(8,128)(2,1)}), bf16[2560,384]{1,0:T(8,128)(2,1)}) %all-gather.9.cloned.1.call-update) | async-done | bytes 1966096 | tf_op jit(solution)/shard_map/all_gather | solution.py:80
  438.7 7.3 %fusion.11 = f32[2560,512]{1,0:T(8,128)} fusion(bf16[2560,384]{1,0:T(8,128)(2,1)} %all-gather.9.cloned.1.call-done, bf16[512,2560]{1,0:T(8,128)(2,1)S(1)} %copy-done, f32[2560]{0:T(1024)S(1)} %copy-done.7, bf16[384,2560]{0,1:T(8,128)(2,1)} %all-gather.7.cloned.1.call-done, f32[384,512]{1,0:T(8,128)} %copy-done.1, pred[512]{0:T(512)(128)(4,1)S(1)} %add_compare_fusion), kind=kOutput, calls=%fused_computation.19 | convolution fusion | flops 2017394688 | bytes 12593664 | tf_op jit(solution)/shard_map/dot_general | solution.py:89
  446.1 1.1 copy-done.2
  447.2 5.7 fusion.32
  453.0 71.1 %psum.31 = f32[]{:T(128)} all-reduce(f32[]{:T(128)} %get-tuple-element.211), channel_id=1, replica_groups=mesh['seg'=8,'shard'=16,'tok'=2] {'shard','tok'}, use_global_device_ids=true, to_apply=%region_12.13 | all-reduce | flops 1 | bytes 8 | tf_op jit(solution)/shard_map/psum | solution.py:76
  524.8 69.9 %reduce-scatter.8.cloned.1.call-done = f32[512,1280]{1,0:T(8,128)} async-done(((f32[512,2560]{1,0:T(8,128)}), f32[512,1280]{1,0:T(8,128)}) %reduce-scatter.8.cloned.1.call-update) | async-done | bytes 2621456 | tf_op jit(solution)/shard_map/reduce_scatter | solution.py:93
  (56 shorter events, 15.6 us)
Async XLA Ops:
  7.2 207.4 %copy-start = (bf16[512,2560]{1,0:T(8,128)(2,1)S(1)}, bf16[512,2560]{1,0:T(8,128)(2,1)}, u32[]{:S(2)}) copy-start(bf16[512,2560]{1,0:T(8,128)(2,1)} %param.19) | copy-start | bytes 7864324
  7.2 3.0 copy-start.5
  7.2 3.0 copy-start.6
  7.2 119.6 %all-reduce.4.cloned.1.call-start = ((), (), s32[]{:S(2)}) async-start(), calls=%async_computation.10 | async-start | bytes 7864320 | tf_op jit(solution)/shard_map/psum | solution.py:41
  11.9 114.8 %copy-start.8 = (bf16[1280,160]{0,1:T(8,128)(2,1)S(1)}, bf16[1280,160]{0,1:T(8,128)(2,1)}, u32[]{:S(2)}) copy-start(bf16[1280,160]{0,1:T(8,128)(2,1)} %param.16) | copy-start | bytes 1228804
  12.0 197.6 %all-gather.7.cloned.1.call-start = ((), (), s32[]{:S(2)}) async-start(), calls=%async_computation.3 | async-start | bytes 2088960 | tf_op jit(solution)/shard_map/all_gather | solution.py:45
  126.8 34.0 %copy-start.10 = (s32[8]{0:T(128)S(1)}, s32[8]{0:T(128)}, u32[]{:S(2)}) copy-start(s32[8]{0:T(128)} %param.21) | copy-start | bytes 100
  126.8 82.8 %copy-start.7 = (f32[2560]{0:T(1024)S(1)}, f32[2560]{0:T(1024)}, u32[]{:S(2)}) copy-start(f32[2560]{0:T(1024)} %param.20) | copy-start | bytes 30724
  126.8 82.8 %copy-start.9 = (f32[512]{0:T(512)S(1)}, f32[512]{0:T(512)}, u32[]{:S(2)}) copy-start(f32[512]{0:T(512)} %param.18) | copy-start | bytes 6148
  160.7 139.5 %reduce-scatter.4.cloned.1.call-start = ((), (), s32[]{:S(2)}) async-start(), calls=%async_computation.4 | async-start | bytes 4177920 | tf_op jit(solution)/shard_map/reduce_scatter | solution.py:62
  213.6 0.9 copy-start.1
  218.2 119.5 %all-gather.11.cloned.1.call-start = ((), (), s32[]{:S(2)}) async-start(), calls=%async_computation.8 | async-start | bytes 2211840 | tf_op jit(solution)/shard_map/all_gather | solution.py:11
  300.2 80.5 %all-gather.13.cloned.1.call-start = ((), (), s32[]{:S(2)}) async-start(), calls=%async_computation.9 | async-start | bytes 2211840 | tf_op jit(solution)/shard_map/all_gather | solution.py:11
  304.0 40.9 %copy-start.4 = (f32[160,384]{1,0:T(8,128)S(1)}, f32[160,384]{1,0:T(8,128)}, u32[]{:S(2)}) copy-start(f32[160,384]{1,0:T(8,128)} %reduce-scatter.4.cloned.1.call-done) | copy-start | bytes 737284
  347.2 91.5 %all-gather.9.cloned.1.call-start = ((), (), s32[]{:S(2)}) async-start(), calls=%async_computation.5 | async-start | bytes 2088960 | tf_op jit(solution)/shard_map/all_gather | solution.py:80
  383.7 7.3 %copy-start.3 = (f32[160,384]{1,0:T(8,128)S(1)}, f32[160,384]{1,0:T(8,128)}, u32[]{:S(2)}) copy-start(f32[160,384]{1,0:T(8,128)} %get-tuple-element.212) | copy-start | bytes 737284
  391.7 133.0 %reduce-scatter.6.cloned.1.call-start = ((), (), s32[]{:S(2)}) async-start(), calls=%async_computation.6 | async-start | bytes 7864320 | tf_op jit(solution)/shard_map/reduce_scatter | solution.py:92
  446.1 1.1 copy-start.2
  446.1 148.6 %reduce-scatter.8.cloned.1.call-start = ((), (), s32[]{:S(2)}) async-start(), calls=%async_computation.7 | async-start | bytes 7864320 | tf_op jit(solution)/shard_map/reduce_scatter | solution.py:93
Sparse Core Ops, SparseCore 0:
  12.1 114.6 all-reduce.3
  160.8 48.6 all-gather.6
  218.3 81.8 reduce-scatter.3
  301.9 35.7 all-gather.10
  347.3 33.3 all-gather.12
  391.8 46.8 all-gather.8
  446.2 73.8 reduce-scatter.5
  523.2 71.4 reduce-scatter.7
where the time goes:
time: 603 us
  waiting for transfers between devices  428 us (71%)
  blocking collectives  102 us (17%)
  matrix products  28.5 us (5%)
  other arithmetic  22.2 us (4%)
  between operations  16.1 us (3%)
    psum x1, waiting for transfers between devices, local(): gate_total, up_total = lax.psum((gate_part, up_part), 'shard')  115 us
    reduce_scatter x1, waiting for transfers between devices, local(): lax.psum_scatter(lax.dot_general(columns, latent_codes, (((0,), (1,)), ((...  82 us
    psum x1, blocking collectives, local(): total_square = lax.psum(jnp.sum(errors * errors), ('shard', 'tok'))  71.1 us
    reduce_scatter x1, waiting for transfers between devices, local(): lax.psum_scatter(grad_piece, 'tok', scatter_dimension=1, tiled=True)  69.9 us
    all_gather x2, waiting for transfers between devices, carried_in(): pieces = lax.all_gather(value, axis)  67.1 us
    all_gather x1, waiting for transfers between devices, local(): mlp_full = lax.all_gather(mlp_slice, 'shard', axis=1, tiled=True)  47.5 us
    all_gather x1, waiting for transfers between devices, local(): piece = lax.all_gather(back, 'shard', axis=0, tiled=True)  47 us
    psum x1, blocking collectives, local(): mlp_slice = lax.psum(down_part, 'seg').astype(jnp.bfloat16)  30.9 us
  transfers between devices with their start and end apart: 8, of which 7 were waited for; matrix products, arithmetic and copies ran while one was open for 2% of the time, Pallas kernels for 0%

commit v1 on v0

v1 whole, which is shorter than its diff:
```python
import math

import jax
import jax.numpy as jnp
from jax import lax
from jax.sharding import PartitionSpec as P

F32 = jnp.float32
BF16 = jnp.bfloat16


def dot(left, right, left_dim, right_dim):
    return lax.dot_general(
        left, right, (((left_dim,), (right_dim,)), ((), ())), preferred_element_type=F32
    )


def core_swap(value):
    count = lax.axis_size("seg")
    return lax.ppermute(value, "seg", [(i, i ^ 1) for i in range(count)])


def chip_shift(value, step):
    count = lax.axis_size("seg")
    return lax.ppermute(value, "seg", [(i, (i + 2 * step) % count) for i in range(count)])


def shard_shift(value, axis, step):
    pairs = []
    for x in range(4):
        for y in range(4):
            to = ((x + step) % 4, y) if axis == 0 else (x, (y + step) % 4)
            pairs.append((4 * x + y, 4 * to[0] + to[1]))
    return lax.ppermute(value, "shard", pairs)


def tok_swap(value):
    return lax.ppermute(value, "tok", [(0, 1), (1, 0)])


def shard_exchange(pieces):
    return lax.all_to_all(pieces, "shard", 0, 0)


def shard_gather(value):
    count = lax.axis_size("shard")
    return shard_exchange(jnp.broadcast_to(value[None], (count,) + value.shape))


def local(
    activations,
    gate_weight,
    up_weight,
    down_weight,
    encoder_weight,
    encoder_bias,
    decoder_weight,
    decoder_bias,
    segment_sizes,
):
    shard_index = lax.axis_index("shard")
    segment_index = lax.axis_index("seg")
    tok_index = lax.axis_index("tok")
    core = segment_index % 2
    shards = lax.axis_size("shard")
    tokens, width_slice = activations.shape
    tokens_all = tokens * lax.axis_size("tok")
    width = decoder_bias.shape[0]
    half = width // 2
    segment_total = segment_sizes.shape[0]

    gate_part = dot(gate_weight, activations, 0, 1).reshape(shards, -1, tokens)
    up_part = dot(up_weight, activations, 0, 1).reshape(shards, -1, tokens)
    both = jnp.concatenate([gate_part.astype(BF16), up_part.astype(BF16)], axis=1)
    both = jnp.sum(shard_exchange(both).astype(F32), axis=0)
    units = both.shape[0] // 2
    hidden_slice = (jax.nn.gelu(both[:units], approximate=True) * both[units:]).astype(BF16)
    hidden = shard_gather(hidden_slice).reshape(-1, tokens)
    down_part = dot(down_weight, hidden, 0, 0).reshape(2, -1, tokens)
    kept = lax.dynamic_index_in_dim(down_part, core, 0, keepdims=False)
    given = lax.dynamic_index_in_dim(down_part, 1 - core, 0, keepdims=False)
    pair_sum = kept + core_swap(given)
    pair_sent = pair_sum.astype(BF16)
    total = pair_sum
    for step in (1, 2, 3):
        total = total + chip_shift(pair_sent, step).astype(F32)
    mine = shard_gather(total.astype(BF16))
    other = core_swap(mine)
    mlp_full = jnp.where(
        core == 0, jnp.stack([mine, other], axis=1), jnp.stack([other, mine], axis=1)
    ).reshape(width, tokens)
    centered = (mlp_full.astype(F32) - decoder_bias[:, None]).astype(BF16)
    centered_other = tok_swap(lax.dynamic_slice_in_dim(centered, (1 - tok_index) * half, half, 0))

    lat_count = encoder_weight.shape[1]
    size_here = jnp.sum(jnp.where(jnp.arange(segment_total) == segment_index, segment_sizes, 0))
    latent_index = shard_index * lat_count + jnp.arange(lat_count)
    live_mask = (latent_index < size_here)[:, None]
    pre_act = dot(encoder_weight, centered, 0, 0) + encoder_bias[:, None]
    codes = jnp.where(live_mask, jax.nn.softplus(10.0 * pre_act) / 10.0, 0.0).astype(BF16)
    slope = jnp.where(live_mask, jax.nn.sigmoid(10.0 * pre_act), 0.0)
    codes_other = tok_swap(codes)

    part = dot(decoder_weight, codes, 0, 0).astype(BF16).reshape(shards, width_slice, tokens)
    my_part = jnp.sum(shard_exchange(part).astype(F32), axis=0)
    parts = lax.all_gather(my_part.astype(BF16), "seg").astype(F32)
    start = shard_index * width_slice
    target = lax.dynamic_slice_in_dim(mlp_full, start, width_slice, 0).astype(F32)
    bias_slice = lax.dynamic_slice_in_dim(decoder_bias, start, width_slice, 0)[:, None]
    base = bias_slice - target
    places = jnp.arange(segment_total)
    up_to = (places <= segment_index).astype(F32)[:, None, None]
    weight = (segment_total - jnp.maximum(places, segment_index)).astype(F32)[:, None, None]
    errors = base + jnp.sum(parts * up_to, axis=0)
    summed = (segment_total - segment_index).astype(F32) * base + jnp.sum(parts * weight, axis=0)
    back_slice = (summed * (1.0 / math.sqrt(tokens_all))).astype(BF16)

    square = jnp.broadcast_to(jnp.sum(errors * errors), (8, 128))
    for axis in (0, 1):
        moved = [shard_shift(square, axis, step) for step in (1, 2, 3)]
        square = square + moved[0] + moved[1] + moved[2]
    square = square + tok_swap(square)
    prefix_mse = square[0, :1] / (tokens_all * width)

    back = shard_gather(back_slice).reshape(width, tokens)
    back_other = tok_swap(lax.dynamic_slice_in_dim(back, (1 - tok_index) * half, half, 0))
    code_acc = dot(decoder_weight, back, 1, 0)
    code_grad = (code_acc * slope).astype(BF16)
    code_grad_other = tok_swap(code_grad)
    back_mine = lax.dynamic_slice_in_dim(back, tok_index * half, half, 0)
    centered_mine = lax.dynamic_slice_in_dim(centered, tok_index * half, half, 0)
    grad_decoder = dot(codes, back_mine, 1, 1) + dot(codes_other, back_other, 1, 1)
    grad_encoder = dot(centered_mine, code_grad, 1, 1) + dot(
        centered_other, code_grad_other, 1, 1
    )
    return (grad_encoder, grad_decoder, prefix_mse)


def solution(mesh):
    in_specs = (
        P("tok", "shard"),
        P("shard", "seg"),
        P("shard", "seg"),
        P("seg", "shard"),
        P(None, ("seg", "shard")),
        P(("seg", "shard")),
        P(("seg", "shard"), None),
        P(),
        P(),
    )
    out_specs = (P("tok", ("seg", "shard")), P(("seg", "shard"), "tok"), P("seg"))
    return jax.shard_map(local, mesh=mesh, in_specs=in_specs, out_specs=out_specs, check_vma=False)
```

time: 603 us -> 274 us (0.45)
  waiting for transfers between devices: 428 us -> 113 us
  starting transfers between devices: 0.33 us -> 38.6 us
  blocking collectives: 102 us -> 71.7 us
  between operations: 16.1 us -> 2.68 us
  other arithmetic: 22.2 us -> 9.44 us
  local copies, waits for them, and re-layouts: 5.01 us -> 13.5 us
  matrix products: 28.5 us -> 21.7 us
    all_gather x4 -> x0, waiting for transfers between devices: 162 us -> none  [the longest x2 67.1 us: carried_in(): pieces = lax.all_gather(value, axis)]
    reduce_scatter x3 -> x0, waiting for transfers between devices: 152 us -> none  [the longest x1 82 us: local(): lax.psum_scatter(lax.dot_general(columns, latent_codes, (((0,), (1,)), ((...]
    psum x1 -> x0, waiting for transfers between devices: 115 us -> none  [local(): gate_total, up_total = lax.psum((gate_part, up_part), 'shard')]
    psum x2 -> x0, blocking collectives: 102 us -> none  [the longest x1 71.1 us: local(): total_square = lax.psum(jnp.sum(errors * errors), ('shard', 'tok'))]
    ppermute x0 -> x16, waiting for transfers between devices: none -> 71.6 us  [the longest x5 38.4 us: tok_swap(): return lax.ppermute(value, 'tok', [(0, 1), (1, 0)])]
    all_to_all x0 -> x2, blocking collectives: none -> 50.2 us  [shard_exchange(): return lax.all_to_all(pieces, 'shard', 0, 0)]
    all_to_all x0 -> x3, waiting for transfers between devices: none -> 41.8 us  [shard_exchange(): return lax.all_to_all(pieces, 'shard', 0, 0)]
    ppermute x0 -> x16, starting transfers between devices: none -> 25.4 us  [the longest x3 9.34 us: chip_shift(): lax.ppermute(value, 'seg', [(i, (i + 2 * step) % count) for i in range(co...]
  transfers between devices with their start and end apart: 8 -> 19, of which waited for: 7 -> 14; matrix products, arithmetic and copies ran while one was open for 2% -> 6% of each run, Pallas kernels for 0% -> 0%
where the time goes in v1:
time: 274 us; the launch traced here: 271 us
  waiting for transfers between devices  113 us (41%)
  blocking collectives  71.7 us (26%)
  starting transfers between devices  38.6 us (14%)
  matrix products  21.7 us (8%)
  local copies, waits for them, and re-layouts  13.5 us (5%)
  other arithmetic  9.44 us (3%)
    all_to_all x2, blocking collectives, shard_exchange(): return lax.all_to_all(pieces, 'shard', 0, 0)  50.2 us
    all_to_all x3, waiting for transfers between devices, shard_exchange(): return lax.all_to_all(pieces, 'shard', 0, 0)  41.8 us
    ppermute x5, waiting for transfers between devices, tok_swap(): return lax.ppermute(value, 'tok', [(0, 1), (1, 0)])  38.4 us
    ppermute x6, waiting for transfers between devices, shard_shift(): return lax.ppermute(value, 'shard', pairs)  26.4 us
    dot_general x10, matrix products, dot(): lax.dot_general(left, right, (((left_dim,), (right_dim,)), ((), ())), pre...  21.7 us
    all_gather x1, blocking collectives, local(): parts = lax.all_gather(my_part.astype(BF16), 'seg').astype(F32)  21.5 us
    all_to_all x3, starting transfers between devices, shard_exchange(): return lax.all_to_all(pieces, 'shard', 0, 0)  13.2 us
    ppermute x3, starting transfers between devices, chip_shift(): lax.ppermute(value, 'seg', [(i, (i + 2 * step) % count) for i in range(co...  9.34 us
  transfers between devices with their start and end apart: 19, of which 14 were waited for; matrix products, arithmetic and copies ran while one was open for 6% of the time, Pallas kernels for 0%

profile of v1, /device:TPU:1, one launch (start us, length us, event | category | flops | bytes accessed | tf_op | source)
XLA Modules:
  0.0 271.0 jit_solution(5994261272490255571)
XLA Ops:
  4.2 32.7 %all_to_all.25 = bf16[16,160,384]{2,1,0:T(8,128)(2,1)S(1)} all-to-all(bf16[16,160,384]{2,1,0:T(8,128)(2,1)S(1)} %pad_maximum_fusion), channel_id=1, replica_groups=mesh['seg'=8,'shard'=16,'tok'=2] {'shard'}, dimensions={0} | all-to-all | bytes 3932160 | tf_op jit(solution)/shard_map/all_to_all | solution.py:42
  38.3 4.3 %all-to-all-start.1 = ((bf16[16,80,384]{2,1,0:T(8,128)(2,1)}), bf16[16,80,384]{2,1,0:T(8,128)(2,1)}, u32[]{:S(2)}, u32[]{:S(2)}) async-start(bf16[16,80,384]{2,1,0:T(8,128)(2,1)} %broadcast_in_dim.26), calls=%async_computation.1 | async-start | bytes 1966080 | tf_op jit(solution)/shard_map/all_to_all | solution.py:42
  42.6 14.1 %all-to-all-done.1 = bf16[16,80,384]{2,1,0:T(8,128)(2,1)} async-done(((bf16[16,80,384]{2,1,0:T(8,128)(2,1)}), bf16[16,80,384]{2,1,0:T(8,128)(2,1)}, u32[]{:S(2)}, u32[]{:S(2)}) %all-to-all-start.1) | async-done | bytes 983072 | tf_op jit(solution)/shard_map/all_to_all | solution.py:42
  58.3 3.4 %collective-permute-start = (f32[80,384]{1,0:T(8,128)S(1)}, f32[80,384]{1,0:T(8,128)S(1)}, u32[]{:S(2)}, u32[]{:S(2)}) collective-permute-start(f32[80,384]{1,0:T(8,128)S(1)} %dynamic-slice_bitcast_fusion), channel_id=1, source_target_pairs={{0,32},{32,0},{64,96},{96,64},{128,160},{160,128},{192,224},{224,1... | collective-permute-start | bytes 368648 | tf_op jit(solution)/shard_map/ppermute | solution.py:20
  62.7 6.1 %collective-permute-start.3 = (bf16[80,384]{1,0:T(8,128)(2,1)S(1)}, bf16[80,384]{1,0:T(8,128)(2,1)S(1)}, u32[]{:S(2)}, u32[]{:S(2)}) collective-permute-start(bf16[80,384]{1,0:T(8,128)(2,1)S(1)} %fusion.23), channel_id=1, source_target_pairs={{0,192},{32,224},{64,0},{96,32},{128,64},{160,96},{192,128},{224,1... | collective-permute-start | bytes 184328 | tf_op jit(solution)/shard_map/ppermute | solution.py:25
  72.1 3.9 %collective-permute-done.2 = bf16[80,384]{1,0:T(8,128)(2,1)S(1)} collective-permute-done((bf16[80,384]{1,0:T(8,128)(2,1)S(1)}, bf16[80,384]{1,0:T(8,128)(2,1)S(1)}, u32[]{:S(2)}, u32[]{:S(2)}) %collective-permute-start.2) | collective-permute-done | bytes 61472 | tf_op jit(solution)/shard_map/ppermute | solution.py:25
  76.8 17.5 %all_to_all.26 = bf16[16,80,384]{2,1,0:T(8,128)(2,1)} all-to-all(bf16[16,80,384]{2,1,0:T(8,128)(2,1)S(1)} %broadcast_in_dim.27), channel_id=1, replica_groups=mesh['seg'=8,'shard'=16,'tok'=2] {'shard'}, dimensions={0} | all-to-all | bytes 1966080 | tf_op jit(solution)/shard_map/all_to_all | solution.py:42
  94.3 3.2 %collective-permute-start.4 = (bf16[16,80,384]{2,1,0:T(8,128)(2,1)}, bf16[16,80,384]{2,1,0:T(8,128)(2,1)}, u32[]{:S(2)}, u32[]{:S(2)}) collective-permute-start(bf16[16,80,384]{2,1,0:T(8,128)(2,1)} %all_to_all.26), channel_id=1, source_target_pairs={{0,32},{32,0},{64,96},{96,64},{128,160},{160,128},{192,224},{224,1... | collective-permute-start | bytes 2949128 | tf_op jit(solution)/shard_map/ppermute | solution.py:20
  100.0 2.5 maximum_select_fusion
  105.0 2.6 fusion.13
  110.0 3.9 %copy.13 = bf16[2560,384]{1,0:T(8,128)(2,1)} copy(bf16[2560,384]{0,1:T(8,128)(2,1)} %fusion) | data formatting | bytes 3932160 | tf_op jit(solution)/shard_map/convert_element_type | solution.py:104
  113.9 4.4 %all-to-all-start.3 = ((bf16[16,160,384]{2,1,0:T(8,128)(2,1)}), bf16[16,160,384]{2,1,0:T(8,128)(2,1)}, u32[]{:S(2)}, u32[]{:S(2)}) async-start(bf16[16,160,384]{2,1,0:T(8,128)(2,1)} %bitcast.52), calls=%async_computation.3 | async-start | bytes 3932160 | tf_op jit(solution)/shard_map/all_to_all | solution.py:42
  118.5 27.7 %all-to-all-done.3 = bf16[16,160,384]{2,1,0:T(8,128)(2,1)} async-done(((bf16[16,160,384]{2,1,0:T(8,128)(2,1)}), bf16[16,160,384]{2,1,0:T(8,128)(2,1)}, u32[]{:S(2)}, u32[]{:S(2)}) %all-to-all-start.3) | async-done | bytes 1966112 | tf_op jit(solution)/shard_map/all_to_all | solution.py:42
  148.0 21.5 %all-gather = bf16[1280,384]{1,0:T(8,128)(2,1)S(1)} all-gather(bf16[160,384]{1,0:T(8,128)(2,1)S(1)} %reduce_sum.59), channel_id=2, replica_groups=mesh['seg'=8,'shard'=16,'tok'=2] {'seg'}, dimensions={0}, use_global_device_ids=true | all-gather | bytes 1105920 | tf_op jit(solution)/shard_map/all_gather | solution.py:106
  173.1 4.4 %all-to-all-start.4 = ((bf16[16,160,384]{2,1,0:T(8,128)(2,1)}), bf16[16,160,384]{2,1,0:T(8,128)(2,1)}, u32[]{:S(2)}, u32[]{:S(2)}) async-start(bf16[16,160,384]{2,1,0:T(8,128)(2,1)} %broadcast_in_dim.49), calls=%async_computation.4 | async-start | bytes 3932160 | tf_op jit(solution)/shard_map/all_to_all | solution.py:42
  178.2 2.7 %collective-permute-start.11 = (f32[8,128]{1,0:T(8,128)S(1)}, f32[8,128]{1,0:T(8,128)S(1)}, u32[]{:S(2)}, u32[]{:S(2)}) collective-permute-start(f32[8,128]{1,0:T(8,128)S(1)} %broadcast_in_dim.50), channel_id=1, source_target_pairs={{0,24},{2,26},{4,28},{6,30},{8,0},{10,2},{12,4},{14,6},{16,8},{18,... | collective-permute-start | bytes 12296 | tf_op jit(solution)/shard_map/ppermute | solution.py:34
  182.0 19.2 %collective-permute-done.11 = f32[8,128]{1,0:T(8,128)S(1)} collective-permute-done((f32[8,128]{1,0:T(8,128)S(1)}, f32[8,128]{1,0:T(8,128)S(1)}, u32[]{:S(2)}, u32[]{:S(2)}) %collective-permute-start.11) | collective-permute-done | bytes 4128 | tf_op jit(solution)/shard_map/ppermute | solution.py:34
  201.3 3.4 %collective-permute-done.10 = f32[8,128]{1,0:T(8,128)S(1)} collective-permute-done((f32[8,128]{1,0:T(8,128)S(1)}, f32[8,128]{1,0:T(8,128)S(1)}, u32[]{:S(2)}, u32[]{:S(2)}) %collective-permute-start.10) | collective-permute-done | bytes 4128 | tf_op jit(solution)/shard_map/ppermute | solution.py:34
  208.1 2.5 collective-permute-done.13
  217.5 3.0 %fusion.6 = bf16[512,384]{0,1:T(8,128)(2,1)S(1)} fusion(bf16[2560,384]{1,0:T(8,128)(2,1)} %bitcast.15, bf16[512,2560]{1,0:T(8,128)(2,1)S(1)} %copy-done, f32[512,384]{0,1:T(8,128)} %get-tuple-element.8, pred[512]{0:T(512)(128)(4,1)S(1)} %add_compare_fusion), kind=kOutput, calls=%fused_computation.20 | convolution fusion | flops 1007812608 | bytes 5767680 | tf_op jit(solution)/shard_map/dot_general | solution.py:13
  226.4 11.7 %collective-permute-done.5 = bf16[1280,384]{1,0:T(8,128)(2,1)} collective-permute-done((bf16[1280,384]{1,0:T(8,128)(2,1)}, bf16[1280,384]{1,0:T(8,128)(2,1)}, u32[]{:S(2)}, u32[]{:S(2)}) %collective-permute-start.5) | collective-permute-done | bytes 983072 | tf_op jit(solution)/shard_map/ppermute | solution.py:38
  238.1 8.3 %collective-permute-done.6 = bf16[512,384]{0,1:T(8,128)(2,1)S(1)} collective-permute-done((bf16[512,384]{0,1:T(8,128)(2,1)S(1)}, bf16[512,384]{0,1:T(8,128)(2,1)S(1)}, u32[]{:S(2)}, u32[]{:S(2)}) %collective-permute-start.6) | collective-permute-done | bytes 393248 | tf_op jit(solution)/shard_map/ppermute | solution.py:38
  246.4 3.5 %convolution_add_fusion.1 = f32[1280,512]{1,0:T(8,128)} fusion(f32[1280,512]{1,0:T(8,128)S(1)} %fusion.9, bf16[1280,384]{1,0:T(8,128)(2,1)} %collective-permute-done.5, bf16[512,384]{0,1:T(8,128)(2,1)S(1)} %collective-permute-done.6), kind=kOutput, calls=%fused_computation.5 | convolution fusion | flops 503971840 | bytes 6619136 | tf_op jit(solution)/shard_map/dot_general | solution.py:13
  250.0 17.5 %collective-permute-done.8 = bf16[1280,384]{1,0:T(8,128)(2,1)S(1)} collective-permute-done((bf16[1280,384]{1,0:T(8,128)(2,1)S(1)}, bf16[1280,384]{1,0:T(8,128)(2,1)S(1)}, u32[]{:S(2)}, u32[]{:S(2)}) %collective-permute-start.8) | collective-permute-done | bytes 983072 | tf_op jit(solution)/shard_map/ppermute | solution.py:38
  (72 shorter events, 44.0 us)
Async XLA Ops:
  0.6 106.9 %copy-start = (bf16[512,2560]{1,0:T(8,128)(2,1)S(1)}, bf16[512,2560]{1,0:T(8,128)(2,1)}, u32[]{:S(2)}) copy-start(bf16[512,2560]{1,0:T(8,128)(2,1)} %param.15) | copy-start | bytes 7864324
  37.2 19.5 %copy-start.4 = (bf16[1280,160]{0,1:T(8,128)(2,1)S(1)}, bf16[1280,160]{0,1:T(8,128)(2,1)}, u32[]{:S(2)}) copy-start(bf16[1280,160]{0,1:T(8,128)(2,1)} %param.12) | copy-start | bytes 1228804
  38.3 18.4 %all-to-all-start.1 = ((bf16[16,80,384]{2,1,0:T(8,128)(2,1)}), bf16[16,80,384]{2,1,0:T(8,128)(2,1)}, u32[]{:S(2)}, u32[]{:S(2)}) async-start(bf16[16,80,384]{2,1,0:T(8,128)(2,1)} %broadcast_in_dim.26), calls=%async_computation.1 | async-start | bytes 1966080 | tf_op jit(solution)/shard_map/all_to_all | solution.py:42
  58.3 39.1 %copy-start.8 = (s32[8]{0:T(128)S(1)}, s32[8]{0:T(128)}, u32[]{:S(2)}) copy-start(s32[8]{0:T(128)} %param.17) | copy-start | bytes 100
  58.3 4.4 %collective-permute-start = (f32[80,384]{1,0:T(8,128)S(1)}, f32[80,384]{1,0:T(8,128)S(1)}, u32[]{:S(2)}, u32[]{:S(2)}) collective-permute-start(f32[80,384]{1,0:T(8,128)S(1)} %dynamic-slice_bitcast_fusion), channel_id=1, source_target_pairs={{0,32},{32,0},{64,96},{96,64},{128,160},{160,128},{192,224},{224,1... | collective-permute-start | bytes 368648 | tf_op jit(solution)/shard_map/ppermute | solution.py:20
  62.7 9.3 %collective-permute-start.3 = (bf16[80,384]{1,0:T(8,128)(2,1)S(1)}, bf16[80,384]{1,0:T(8,128)(2,1)S(1)}, u32[]{:S(2)}, u32[]{:S(2)}) collective-permute-start(bf16[80,384]{1,0:T(8,128)(2,1)S(1)} %fusion.23), channel_id=1, source_target_pairs={{0,192},{32,224},{64,0},{96,32},{128,64},{160,96},{192,128},{224,1... | collective-permute-start | bytes 184328 | tf_op jit(solution)/shard_map/ppermute | solution.py:25
  68.8 7.2 %collective-permute-start.2 = (bf16[80,384]{1,0:T(8,128)(2,1)S(1)}, bf16[80,384]{1,0:T(8,128)(2,1)S(1)}, u32[]{:S(2)}, u32[]{:S(2)}) collective-permute-start(bf16[80,384]{1,0:T(8,128)(2,1)S(1)} %fusion.23), channel_id=1, source_target_pairs={{0,128},{32,160},{64,192},{96,224},{128,0},{160,32},{192,64},{224,... | collective-permute-start | bytes 184328 | tf_op jit(solution)/shard_map/ppermute | solution.py:25
  69.8 6.9 %collective-permute-start.1 = (bf16[80,384]{1,0:T(8,128)(2,1)S(1)}, bf16[80,384]{1,0:T(8,128)(2,1)S(1)}, u32[]{:S(2)}, u32[]{:S(2)}) collective-permute-start(bf16[80,384]{1,0:T(8,128)(2,1)S(1)} %fusion.23), channel_id=1, source_target_pairs={{0,64},{32,96},{64,128},{96,160},{128,192},{160,224},{192,0},{224,... | collective-permute-start | bytes 184328 | tf_op jit(solution)/shard_map/ppermute | solution.py:25
  94.3 5.7 %collective-permute-start.4 = (bf16[16,80,384]{2,1,0:T(8,128)(2,1)}, bf16[16,80,384]{2,1,0:T(8,128)(2,1)}, u32[]{:S(2)}, u32[]{:S(2)}) collective-permute-start(bf16[16,80,384]{2,1,0:T(8,128)(2,1)} %all_to_all.26), channel_id=1, source_target_pairs={{0,32},{32,0},{64,96},{96,64},{128,160},{160,128},{192,224},{224,1... | collective-permute-start | bytes 2949128 | tf_op jit(solution)/shard_map/ppermute | solution.py:20
  105.0 2.6 copy-start.2
  113.9 32.2 %all-to-all-start.3 = ((bf16[16,160,384]{2,1,0:T(8,128)(2,1)}), bf16[16,160,384]{2,1,0:T(8,128)(2,1)}, u32[]{:S(2)}, u32[]{:S(2)}) async-start(bf16[16,160,384]{2,1,0:T(8,128)(2,1)} %bitcast.52), calls=%async_computation.3 | async-start | bytes 3932160 | tf_op jit(solution)/shard_map/all_to_all | solution.py:42
  173.1 44.4 %all-to-all-start.4 = ((bf16[16,160,384]{2,1,0:T(8,128)(2,1)}), bf16[16,160,384]{2,1,0:T(8,128)(2,1)}, u32[]{:S(2)}, u32[]{:S(2)}) async-start(bf16[16,160,384]{2,1,0:T(8,128)(2,1)} %broadcast_in_dim.49), calls=%async_computation.4 | async-start | bytes 3932160 | tf_op jit(solution)/shard_map/all_to_all | solution.py:42
  178.2 23.1 %collective-permute-start.11 = (f32[8,128]{1,0:T(8,128)S(1)}, f32[8,128]{1,0:T(8,128)S(1)}, u32[]{:S(2)}, u32[]{:S(2)}) collective-permute-start(f32[8,128]{1,0:T(8,128)S(1)} %broadcast_in_dim.50), channel_id=1, source_target_pairs={{0,24},{2,26},{4,28},{6,30},{8,0},{10,2},{12,4},{14,6},{16,8},{18,... | collective-permute-start | bytes 12296 | tf_op jit(solution)/shard_map/ppermute | solution.py:34
  180.9 23.8 %collective-permute-start.10 = (f32[8,128]{1,0:T(8,128)S(1)}, f32[8,128]{1,0:T(8,128)S(1)}, u32[]{:S(2)}, u32[]{:S(2)}) collective-permute-start(f32[8,128]{1,0:T(8,128)S(1)} %broadcast_in_dim.50), channel_id=1, source_target_pairs={{0,16},{2,18},{4,20},{6,22},{8,24},{10,26},{12,28},{14,30},{16,0},... | collective-permute-start | bytes 12296 | tf_op jit(solution)/shard_map/ppermute | solution.py:34
  181.4 23.3 %collective-permute-start.9 = (f32[8,128]{1,0:T(8,128)S(1)}, f32[8,128]{1,0:T(8,128)S(1)}, u32[]{:S(2)}, u32[]{:S(2)}) collective-permute-start(f32[8,128]{1,0:T(8,128)S(1)} %broadcast_in_dim.50), channel_id=1, source_target_pairs={{0,8},{2,10},{4,12},{6,14},{8,16},{10,18},{12,20},{14,22},{16,24},... | collective-permute-start | bytes 12296 | tf_op jit(solution)/shard_map/ppermute | solution.py:34
  205.4 2.7 %collective-permute-start.14 = (f32[8,128]{1,0:T(8,128)S(1)}, f32[8,128]{1,0:T(8,128)S(1)}, u32[]{:S(2)}, u32[]{:S(2)}) collective-permute-start(f32[8,128]{1,0:T(8,128)S(1)} %add_add_fusion.1), channel_id=1, source_target_pairs={{0,6},{2,0},{4,2},{6,4},{8,14},{10,8},{12,10},{14,12},{16,22},{18,... | collective-permute-start | bytes 12296 | tf_op jit(solution)/shard_map/ppermute | solution.py:34
  206.7 4.0 %collective-permute-start.13 = (f32[8,128]{1,0:T(8,128)S(1)}, f32[8,128]{1,0:T(8,128)S(1)}, u32[]{:S(2)}, u32[]{:S(2)}) collective-permute-start(f32[8,128]{1,0:T(8,128)S(1)} %add_add_fusion.1), channel_id=1, source_target_pairs={{0,4},{2,6},{4,0},{6,2},{8,12},{10,14},{12,8},{14,10},{16,20},{18,... | collective-permute-start | bytes 12296 | tf_op jit(solution)/shard_map/ppermute | solution.py:34
  208.1 3.7 %collective-permute-start.12 = (f32[8,128]{1,0:T(8,128)S(1)}, f32[8,128]{1,0:T(8,128)S(1)}, u32[]{:S(2)}, u32[]{:S(2)}) collective-permute-start(f32[8,128]{1,0:T(8,128)S(1)} %add_add_fusion.1), channel_id=1, source_target_pairs={{0,2},{2,4},{4,6},{6,0},{8,10},{10,12},{12,14},{14,8},{16,18},{18,... | collective-permute-start | bytes 12296 | tf_op jit(solution)/shard_map/ppermute | solution.py:34
  208.1 41.9 %collective-permute-start.7 = (bf16[512,384]{0,1:T(8,128)(2,1)S(1)}, bf16[512,384]{0,1:T(8,128)(2,1)S(1)}, u32[]{:S(2)}, u32[]{:S(2)}) collective-permute-start(bf16[512,384]{0,1:T(8,128)(2,1)S(1)} %get-tuple-element.7), channel_id=1, source_target_pairs={{0,1},{1,0},{2,3},{3,2},{4,5},{5,4},{6,7},{7,6},{8,9},{9,8},{10,11... | collective-permute-start | bytes 1179656 | tf_op jit(solution)/shard_map/ppermute | solution.py:38
  211.8 4.5 %collective-permute-start.15 = (f32[8,128]{1,0:T(8,128)S(1)}, f32[8,128]{1,0:T(8,128)S(1)}, u32[]{:S(2)}, u32[]{:S(2)}) collective-permute-start(f32[8,128]{1,0:T(8,128)S(1)} %add_add_fusion), channel_id=1, source_target_pairs={{0,1},{1,0},{2,3},{3,2},{4,5},{5,4},{6,7},{7,6},{8,9},{9,8},{10,11... | collective-permute-start | bytes 12296 | tf_op jit(solution)/shard_map/ppermute | solution.py:38
  214.0 24.1 %collective-permute-start.5 = (bf16[1280,384]{1,0:T(8,128)(2,1)}, bf16[1280,384]{1,0:T(8,128)(2,1)}, u32[]{:S(2)}, u32[]{:S(2)}) collective-permute-start(bf16[1280,384]{1,0:T(8,128)(2,1)} %constant_dynamic-slice_fusion.1), channel_id=1, source_target_pairs={{0,1},{1,0},{2,3},{3,2},{4,5},{5,4},{6,7},{7,6},{8,9},{9,8},{10,11... | collective-permute-start | bytes 2949128 | tf_op jit(solution)/shard_map/ppermute | solution.py:38
  220.5 3.0 %copy-start.3 = (bf16[2560,384]{1,0:T(8,128)(2,1)S(1)}, bf16[2560,384]{1,0:T(8,128)(2,1)}, u32[]{:S(2)}) copy-start(bf16[2560,384]{1,0:T(8,128)(2,1)} %copy-done.2) | copy-start | bytes 5898244
  220.5 25.9 %collective-permute-start.6 = (bf16[512,384]{0,1:T(8,128)(2,1)S(1)}, bf16[512,384]{0,1:T(8,128)(2,1)S(1)}, u32[]{:S(2)}, u32[]{:S(2)}) collective-permute-start(bf16[512,384]{0,1:T(8,128)(2,1)S(1)} %fusion.6), channel_id=1, source_target_pairs={{0,1},{1,0},{2,3},{3,2},{4,5},{5,4},{6,7},{7,6},{8,9},{9,8},{10,11... | collective-permute-start | bytes 1179656 | tf_op jit(solution)/shard_map/ppermute | solution.py:38
  222.4 45.1 %collective-permute-start.8 = (bf16[1280,384]{1,0:T(8,128)(2,1)S(1)}, bf16[1280,384]{1,0:T(8,128)(2,1)S(1)}, u32[]{:S(2)}, u32[]{:S(2)}) collective-permute-start(bf16[1280,384]{1,0:T(8,128)(2,1)S(1)} %constant_dynamic-slice_fusion), channel_id=1, source_target_pairs={{0,1},{1,0},{2,3},{3,2},{4,5},{5,4},{6,7},{7,6},{8,9},{9,8},{10,11... | collective-permute-start | bytes 2949128 | tf_op jit(solution)/shard_map/ppermute | solution.py:38
  (4 other events, 8.7 us)

commit v2 on v1

v2 whole, which is shorter than its diff:
```python
import math

import jax
import jax.numpy as jnp
from jax import lax
from jax.experimental.layout import Layout, with_layout_constraint
from jax.sharding import PartitionSpec as P


F32 = jnp.float32
BF16 = jnp.bfloat16


def dot(left, right, left_dim, right_dim):
    return lax.dot_general(
        left, right, (((left_dim,), (right_dim,)), ((), ())), preferred_element_type=F32
    )


def core_swap(value):
    count = lax.axis_size("seg")
    return lax.ppermute(value, "seg", [(i, i ^ 1) for i in range(count)])


def chip_shift(value, step):
    count = lax.axis_size("seg")
    return lax.ppermute(value, "seg", [(i, (i + 2 * step) % count) for i in range(count)])


def tok_swap(value):
    return lax.ppermute(value, "tok", [(0, 1), (1, 0)])


def shard_exchange(pieces):
    return lax.all_to_all(pieces, "shard", 0, 0)


def shard_sum(pieces):
    return jnp.sum(shard_exchange(pieces).astype(F32), axis=0)


def shard_gather(value):
    count = lax.axis_size("shard")
    return shard_exchange(jnp.broadcast_to(value[None], (count,) + value.shape))


def step(
    activations,
    gate_weight,
    up_weight,
    down_weight,
    encoder_weight,
    encoder_bias,
    decoder_weight,
    decoder_bias,
    segment_sizes,
):
    shard_index = lax.axis_index("shard")
    segment_index = lax.axis_index("seg")
    tok_index = lax.axis_index("tok")
    core = segment_index % 2
    shards = lax.axis_size("shard")
    tokens, width_slice = activations.shape
    tokens_all = tokens * lax.axis_size("tok")
    width = decoder_bias.shape[0]
    half = width // 2
    segment_total = segment_sizes.shape[0]

    gate_part = dot(gate_weight, activations, 0, 1).reshape(shards, -1, tokens)
    up_part = dot(up_weight, activations, 0, 1).reshape(shards, -1, tokens)
    both = shard_sum(jnp.concatenate([gate_part.astype(BF16), up_part.astype(BF16)], axis=1))
    units = both.shape[0] // 2
    gate, up = both[:units], both[units:]
    hidden_slice = (jax.nn.gelu(gate, approximate=True) * up).astype(BF16)
    hidden = shard_gather(hidden_slice).reshape(-1, tokens)
    down_part = dot(down_weight, hidden, 0, 0).reshape(2, -1, tokens)
    kept = lax.dynamic_index_in_dim(down_part, core, 0, keepdims=False)
    given = lax.dynamic_index_in_dim(down_part, 1 - core, 0, keepdims=False)
    pair_sum = kept + core_swap(given)
    pair_sent = pair_sum.astype(BF16)
    total = pair_sum
    for step in (1, 2, 3):
        total = total + chip_shift(pair_sent, step).astype(F32)
    mine = shard_gather(total.astype(BF16))
    other = core_swap(mine)
    rows = mine.shape[1]

    def by_core(here, there, dim):
        return jnp.where(
            core == 0,
            jnp.concatenate([here, there], axis=dim),
            jnp.concatenate([there, here], axis=dim),
        )

    def half_of(values, which):
        values = values.reshape((shards, 2, rows) + values.shape[1:])
        return lax.dynamic_index_in_dim(values, which, 1, keepdims=False)

    bias_column = decoder_bias[:, None]
    centered_mine = (mine.astype(F32) - half_of(bias_column, core)).astype(BF16)
    centered_other = (other.astype(F32) - half_of(bias_column, 1 - core)).astype(BF16)
    encoder_mine = half_of(encoder_weight, core).reshape(shards * rows, -1)
    encoder_other = half_of(encoder_weight, 1 - core).reshape(shards * rows, -1)

    def tok_half(pieces, which):
        return lax.dynamic_slice_in_dim(pieces, which * (shards // 2), shards // 2, 0)

    target = by_core(
        lax.dynamic_index_in_dim(mine, shard_index, 0, keepdims=False),
        lax.dynamic_index_in_dim(other, shard_index, 0, keepdims=False),
        0,
    ).astype(F32)
    sent = [tok_half(c, 1 - tok_index) for c in (centered_mine, centered_other)]
    centered_peer = tok_swap(jnp.concatenate(sent, axis=0))

    lat_count = encoder_weight.shape[1]
    size_here = jnp.sum(jnp.where(jnp.arange(segment_total) == segment_index, segment_sizes, 0))
    latent_index = shard_index * lat_count + jnp.arange(lat_count)
    live_mask = (latent_index < size_here)[:, None]
    pre_act = dot(encoder_mine, centered_mine.reshape(-1, tokens), 0, 0)
    pre_act = pre_act + dot(encoder_other, centered_other.reshape(-1, tokens), 0, 0)
    pre_act = pre_act + encoder_bias[:, None]
    codes = jnp.where(live_mask, jax.nn.softplus(10.0 * pre_act) / 10.0, 0.0).astype(BF16)
    slope = jnp.where(live_mask, jax.nn.sigmoid(10.0 * pre_act), 0.0)
    codes_other = tok_swap(codes)

    part = dot(decoder_weight, codes, 0, 0).astype(BF16)
    split = 96
    part = with_layout_constraint(part, Layout((0, 1))).reshape(shards, width_slice, tokens)
    start = shard_index * width_slice
    bias_slice = lax.dynamic_slice_in_dim(decoder_bias, start, width_slice, 0)[:, None]
    base = bias_slice - target
    places = jnp.arange(segment_total)
    up_to = (places <= segment_index).astype(F32)[:, None, None]
    weight = (segment_total - jnp.maximum(places, segment_index)).astype(F32)[:, None, None]
    base_weight = (segment_total - segment_index).astype(F32)
    scale = 1.0 / math.sqrt(tokens_all)

    def seg_step(mine, base):
        parts = lax.all_gather(mine, "seg").astype(F32)
        errors = base + jnp.sum(parts * up_to, axis=0)
        summed = base_weight * base + jnp.sum(parts * weight, axis=0)
        return (summed * scale).astype(BF16), jnp.sum(errors * errors, axis=0, keepdims=True)

    sum_first = shard_sum(part[:, :split]).astype(BF16)
    sum_second = shard_sum(part[:, split:]).astype(BF16)
    slice_first, square_first = seg_step(sum_first, base[:split])
    slice_first, square_first, sum_second = lax.optimization_barrier(
        (slice_first, square_first, sum_second)
    )
    back_first = shard_gather(slice_first)
    slice_second, square_second = seg_step(sum_second, base[split:])

    square = square_first + square_second
    high = square.astype(BF16)
    low = (square - high.astype(F32)).astype(BF16)
    row = lax.broadcasted_iota(jnp.int32, (8, tokens), 0)
    extra = jnp.where(row == 0, high, jnp.where(row == 1, low, jnp.zeros_like(low)))
    back_second = shard_gather(jnp.concatenate([slice_second, extra], axis=0))

    def joined(first, second):
        return jnp.concatenate([first, second], axis=1).reshape(-1, tokens)

    first_other = tok_swap(tok_half(back_first, 1 - tok_index))
    rest = width_slice - split
    second_other = tok_swap(
        lax.dynamic_slice(
            back_second,
            ((1 - tok_index) * (shards // 2), 0, 0),
            (shards // 2, rest, tokens),
        )
    )
    back = joined(back_first, back_second[:, :rest])
    code_acc = dot(decoder_weight, back, 1, 0)
    code_grad = (code_acc * slope).astype(BF16)
    code_grad_other = tok_swap(code_grad)

    squares = jnp.broadcast_to(jnp.sum(back_second[:, rest:].astype(F32)), (8, 128))
    squares = squares + tok_swap(squares)
    prefix_mse = squares[0, :1] / (tokens_all * width)

    back_mine = lax.dynamic_slice_in_dim(back, tok_index * half, half, 0)
    back_other = joined(first_other, second_other)
    grad_decoder = dot(codes, back_mine, 1, 1)
    grad_decoder = grad_decoder + dot(codes_other, back_other, 1, 1)
    count = shards // 2
    own = by_core(tok_half(centered_mine, tok_index), tok_half(centered_other, tok_index), 1)
    own = lax.optimization_barrier(own.reshape(half, tokens))
    peer = by_core(centered_peer[:count], centered_peer[count:], 1)
    peer = lax.optimization_barrier(peer.reshape(half, tokens))
    grad_encoder = dot(own, code_grad, 1, 1)
    grad_encoder = grad_encoder + dot(peer, code_grad_other, 1, 1)
    return (grad_encoder, grad_decoder, prefix_mse)


def solution(mesh):
    in_specs = (
        P("tok", "shard"),
        P("shard", "seg"),
        P("shard", "seg"),
        P("seg", "shard"),
        P(None, ("seg", "shard")),
        P(("seg", "shard")),
        P(("seg", "shard"), None),
        P(),
        P(),
    )
    out_specs = (P("tok", ("seg", "shard")), P(("seg", "shard"), "tok"), P("seg"))
    return jax.shard_map(step, mesh=mesh, in_specs=in_specs, out_specs=out_specs, check_vma=False)
```

time: 274 us -> 264 us (0.964)
  waiting for transfers between devices: 113 us -> 73 us
  blocking collectives: 71.7 us -> 86.6 us
  other arithmetic: 9.44 us -> 18.8 us
  local copies, waits for them, and re-layouts: 13.5 us -> 21.5 us
  matrix products: 21.7 us -> 18.6 us
    ppermute x6 -> x0, waiting for transfers between devices: 26.4 us -> none  [shard_shift(): return lax.ppermute(value, 'shard', pairs)]
    ppermute x5 -> x6, waiting for transfers between devices: 38.4 us -> 15.9 us  [tok_swap(): return lax.ppermute(value, 'tok', [(0, 1), (1, 0)])]
    all_gather x1 -> x2, blocking collectives: 21.5 us -> 36.4 us  [seg_step(): parts = lax.all_gather(mine, 'seg').astype(F32)]
    all_to_all x3 -> x5, waiting for transfers between devices: 41.8 us -> 51.5 us  [shard_exchange(): return lax.all_to_all(pieces, 'shard', 0, 0)]
    all_to_all x3 -> x5, starting transfers between devices: 13.2 us -> 20.3 us  [shard_exchange(): return lax.all_to_all(pieces, 'shard', 0, 0)]
    ppermute x6 -> x0, starting transfers between devices: 6.59 us -> none  [shard_shift(): return lax.ppermute(value, 'shard', pairs)]
    slice x1 -> x5, local copies, waits for them, and re-layouts: 0.51 us -> 6.21 us  [the longest x1 2.41 us: step(): sum_first = shard_sum(part[:, :split]).astype(BF16)]
    concatenate x1 -> x5, other arithmetic: 0.2 us -> 5.27 us  [the longest x2 2.81 us: joined(): return jnp.concatenate([first, second], axis=1).reshape(-1, tokens)]
  transfers between devices with their start and end apart: 19 -> 16, of which waited for: 14 -> 12; matrix products, arithmetic and copies ran while one was open for 6% -> 14% of each run, Pallas kernels for 0% -> 0%
where the time goes in v2:
time: 264 us; the launch traced here: 261 us
  blocking collectives  86.6 us (33%)
  waiting for transfers between devices  73 us (28%)
  starting transfers between devices  39.5 us (15%)
  local copies, waits for them, and re-layouts  21.5 us (8%)
  other arithmetic  18.8 us (7%)
  matrix products  18.6 us (7%)
  between operations  2.85 us (1%)
    all_to_all x5, waiting for transfers between devices, shard_exchange(): return lax.all_to_all(pieces, 'shard', 0, 0)  51.5 us
    all_to_all x2, blocking collectives, shard_exchange(): return lax.all_to_all(pieces, 'shard', 0, 0)  50.2 us
    all_gather x2, blocking collectives, seg_step(): parts = lax.all_gather(mine, 'seg').astype(F32)  36.4 us
    all_to_all x5, starting transfers between devices, shard_exchange(): return lax.all_to_all(pieces, 'shard', 0, 0)  20.3 us
    dot_general x11, matrix products, dot(): lax.dot_general(left, right, (((left_dim,), (right_dim,)), ((), ())), pre...  18.6 us
    ppermute x6, waiting for transfers between devices, tok_swap(): return lax.ppermute(value, 'tok', [(0, 1), (1, 0)])  15.9 us
    ppermute x3, starting transfers between devices, chip_shift(): lax.ppermute(value, 'seg', [(i, (i + 2 * step) % count) for i in range(co...  9.34 us
    ppermute x2, starting transfers between devices, core_swap(): return lax.ppermute(value, 'seg', [(i, i ^ 1) for i in range(count)])  6.57 us
  transfers between devices with their start and end apart: 16, of which 12 were waited for; matrix products, arithmetic and copies ran while one was open for 14% of the time, Pallas kernels for 0%

profile of v2, /device:TPU:1, one launch (start us, length us, event | category | flops | bytes accessed | tf_op | source)
XLA Modules:
  0.0 260.8 jit_solution(12968130441430054528)
XLA Ops:
  4.2 32.7 %all_to_all.35 = bf16[16,160,384]{2,1,0:T(8,128)(2,1)S(1)} all-to-all(bf16[16,160,384]{2,1,0:T(8,128)(2,1)S(1)} %pad_maximum_fusion), channel_id=1, replica_groups=mesh['seg'=8,'shard'=16,'tok'=2] {'shard'}, dimensions={0} | all-to-all | bytes 3932160 | tf_op jit(solution)/shard_map/all_to_all | solution.py:35
  38.3 4.3 %all-to-all-start.1 = ((bf16[16,80,384]{2,1,0:T(8,128)(2,1)}), bf16[16,80,384]{2,1,0:T(8,128)(2,1)}, u32[]{:S(2)}, u32[]{:S(2)}) async-start(bf16[16,80,384]{2,1,0:T(8,128)(2,1)} %broadcast_in_dim.85), calls=%async_computation.1 | async-start | bytes 1966080 | tf_op jit(solution)/shard_map/all_to_all | solution.py:35
  42.6 14.1 %all-to-all-done.1 = bf16[16,80,384]{2,1,0:T(8,128)(2,1)} async-done(((bf16[16,80,384]{2,1,0:T(8,128)(2,1)}), bf16[16,80,384]{2,1,0:T(8,128)(2,1)}, u32[]{:S(2)}, u32[]{:S(2)}) %all-to-all-start.1) | async-done | bytes 983072 | tf_op jit(solution)/shard_map/all_to_all | solution.py:35
  58.3 3.4 %collective-permute-start = (f32[80,384]{1,0:T(8,128)S(1)}, f32[80,384]{1,0:T(8,128)S(1)}, u32[]{:S(2)}, u32[]{:S(2)}) collective-permute-start(f32[80,384]{1,0:T(8,128)S(1)} %dynamic-slice_bitcast_fusion), channel_id=1, source_target_pairs={{0,32},{32,0},{64,96},{96,64},{128,160},{160,128},{192,224},{224,1... | collective-permute-start | bytes 368648 | tf_op jit(solution)/shard_map/ppermute | solution.py:22
  62.7 6.1 %collective-permute-start.3 = (bf16[80,384]{1,0:T(8,128)(2,1)S(1)}, bf16[80,384]{1,0:T(8,128)(2,1)S(1)}, u32[]{:S(2)}, u32[]{:S(2)}) collective-permute-start(bf16[80,384]{1,0:T(8,128)(2,1)S(1)} %fusion.22), channel_id=1, source_target_pairs={{0,192},{32,224},{64,0},{96,32},{128,64},{160,96},{192,128},{224,1... | collective-permute-start | bytes 184328 | tf_op jit(solution)/shard_map/ppermute | solution.py:27
  69.8 2.3 collective-permute-start.1
  72.1 3.9 %collective-permute-done.2 = bf16[80,384]{1,0:T(8,128)(2,1)S(1)} collective-permute-done((bf16[80,384]{1,0:T(8,128)(2,1)S(1)}, bf16[80,384]{1,0:T(8,128)(2,1)S(1)}, u32[]{:S(2)}, u32[]{:S(2)}) %collective-permute-start.2) | collective-permute-done | bytes 61472 | tf_op jit(solution)/shard_map/ppermute | solution.py:27
  76.8 17.5 %all_to_all.36 = bf16[16,80,384]{2,1,0:T(8,128)(2,1)} all-to-all(bf16[16,80,384]{2,1,0:T(8,128)(2,1)S(1)} %broadcast_in_dim.86), channel_id=1, replica_groups=mesh['seg'=8,'shard'=16,'tok'=2] {'shard'}, dimensions={0} | all-to-all | bytes 1966080 | tf_op jit(solution)/shard_map/all_to_all | solution.py:35
  94.3 3.2 %collective-permute-start.4 = (bf16[16,80,384]{2,1,0:T(8,128)(2,1)}, bf16[16,80,384]{2,1,0:T(8,128)(2,1)}, u32[]{:S(2)}, u32[]{:S(2)}) collective-permute-start(bf16[16,80,384]{2,1,0:T(8,128)(2,1)} %all_to_all.36), channel_id=1, source_target_pairs={{0,32},{32,0},{64,96},{96,64},{128,160},{160,128},{192,224},{224,1... | collective-permute-start | bytes 2949128 | tf_op jit(solution)/shard_map/ppermute | solution.py:22
  110.8 3.6 %all-to-all-start.4 = ((bf16[16,64,384]{2,1,0:T(8,128)(2,1)}), bf16[16,64,384]{2,1,0:T(8,128)(2,1)S(1)}, u32[]{:S(2)}, u32[]{:S(2)}) async-start(bf16[16,64,384]{2,1,0:T(8,128)(2,1)} %slice.48), calls=%async_computation.4 | async-start | bytes 1572864 | tf_op jit(solution)/shard_map/all_to_all | solution.py:35
  114.4 2.4 slice.47
  116.8 11.8 %all-to-all-done.4 = bf16[16,64,384]{2,1,0:T(8,128)(2,1)S(1)} async-done(((bf16[16,64,384]{2,1,0:T(8,128)(2,1)}), bf16[16,64,384]{2,1,0:T(8,128)(2,1)S(1)}, u32[]{:S(2)}, u32[]{:S(2)}) %all-to-all-start.4) | async-done | bytes 786464 | tf_op jit(solution)/shard_map/all_to_all | solution.py:35
  128.5 4.4 %all-to-all-start.3 = ((bf16[16,96,384]{2,1,0:T(8,128)(2,1)}), bf16[16,96,384]{2,1,0:T(8,128)(2,1)}, u32[]{:S(2)}, u32[]{:S(2)}) async-start(bf16[16,96,384]{2,1,0:T(8,128)(2,1)} %slice.47), calls=%async_computation.3 | async-start | bytes 2359296 | tf_op jit(solution)/shard_map/all_to_all | solution.py:35
  139.0 10.8 %all-to-all-done.3 = bf16[16,96,384]{2,1,0:T(8,128)(2,1)} async-done(((bf16[16,96,384]{2,1,0:T(8,128)(2,1)}), bf16[16,96,384]{2,1,0:T(8,128)(2,1)}, u32[]{:S(2)}, u32[]{:S(2)}) %all-to-all-start.3) | async-done | bytes 1179680 | tf_op jit(solution)/shard_map/all_to_all | solution.py:35
  151.3 21.4 %all-gather = bf16[768,384]{1,0:T(8,128)(2,1)S(1)} all-gather(bf16[96,384]{1,0:T(8,128)(2,1)S(1)} %reduce_sum.107), channel_id=2, replica_groups=mesh['seg'=8,'shard'=16,'tok'=2] {'seg'}, dimensions={0}, use_global_device_ids=true | all-gather | bytes 663552 | tf_op jit(solution)/shard_map/all_gather | solution.py:140
  173.7 15.0 %all-gather.1 = bf16[512,384]{1,0:T(8,128)(2,1)S(1)} all-gather(bf16[64,384]{1,0:T(8,128)(2,1)S(1)} %reduce_sum.111), channel_id=3, replica_groups=mesh['seg'=8,'shard'=16,'tok'=2] {'seg'}, dimensions={0}, use_global_device_ids=true | all-gather | bytes 442368 | tf_op jit(solution)/shard_map/all_gather | solution.py:140
  190.1 3.6 %all-to-all-start.6 = ((bf16[16,72,384]{2,1,0:T(8,128)(2,1)}), bf16[16,72,384]{2,1,0:T(8,128)(2,1)S(1)}, u32[]{:S(2)}, u32[]{:S(2)}) async-start(bf16[16,72,384]{2,1,0:T(8,128)(2,1)} %broadcast_in_dim.97), calls=%async_computation.6 | async-start | bytes 1769472 | tf_op jit(solution)/shard_map/all_to_all | solution.py:35
  196.0 12.8 %all-to-all-done.6 = bf16[16,72,384]{2,1,0:T(8,128)(2,1)S(1)} async-done(((bf16[16,72,384]{2,1,0:T(8,128)(2,1)}), bf16[16,72,384]{2,1,0:T(8,128)(2,1)S(1)}, u32[]{:S(2)}, u32[]{:S(2)}) %all-to-all-start.6) | async-done | bytes 884768 | tf_op jit(solution)/shard_map/all_to_all | solution.py:35
  210.7 4.4 %all-to-all-start.5 = ((bf16[16,96,384]{2,1,0:T(8,128)(2,1)}), bf16[16,96,384]{2,1,0:T(8,128)(2,1)}, u32[]{:S(2)}, u32[]{:S(2)}) async-start(bf16[16,96,384]{2,1,0:T(8,128)(2,1)} %broadcast_in_dim.90), calls=%async_computation.5 | async-start | bytes 2359296 | tf_op jit(solution)/shard_map/all_to_all | solution.py:35
  215.2 2.7 %maximum_select_fusion = bf16[8,160,384]{2,1,0:T(8,128)(2,1)} fusion(bf16[8,80,384]{2,1,0:T(8,128)(2,1)} %get-tuple-element.22, bf16[8,80,384]{2,1,0:T(8,128)(2,1)} %get-tuple-element.20, pred[]{:T(512)S(6)} %eq.25), kind=kLoop, calls=%fused_computation.21 | loop fusion | flops 4423680 | bytes 1966081 | tf_op jit(solution)/shard_map/jit(_where)/select_n | solution.py:89
  239.7 2.9 %collective-permute-done.6 = bf16[512,384]{1,0:T(8,128)(2,1)S(1)} collective-permute-done((bf16[512,384]{1,0:T(8,128)(2,1)S(1)}, bf16[512,384]{1,0:T(8,128)(2,1)S(1)}, u32[]{:S(2)}, u32[]{:S(2)}) %collective-permute-start.6) | collective-permute-done | bytes 393248 | tf_op jit(solution)/shard_map/ppermute | solution.py:31
  242.6 2.4 convolution_add_fusion.1
  245.0 10.2 %collective-permute-done.8 = bf16[8,96,384]{2,1,0:T(8,128)(2,1)S(1)} collective-permute-done((bf16[8,96,384]{2,1,0:T(8,128)(2,1)S(1)}, bf16[8,96,384]{2,1,0:T(8,128)(2,1)S(1)}, u32[]{:S(2)}, u32[]{:S(2)}) %collective-permute-start.8) | collective-permute-done | bytes 589856 | tf_op jit(solution)/shard_map/ppermute | solution.py:31
  256.3 3.4 %convolution_add_fusion = f32[512,1280]{1,0:T(8,128)} fusion(f32[512,1280]{1,0:T(8,128)S(1)} %fusion.6, bf16[512,384]{1,0:T(8,128)(2,1)} %collective-permute-done.7, bf16[1280,384]{1,0:T(8,128)(2,1)S(1)} %bitcast.67), kind=kOutput, calls=%fused_computation.2 | convolution fusion | flops 503971840 | bytes 6619136 | tf_op jit(solution)/shard_map/dot_general | solution.py:15
  (104 shorter events, 58.7 us)
Async XLA Ops:
  0.6 106.3 %copy-start = (bf16[512,2560]{1,0:T(8,128)(2,1)S(1)}, bf16[512,2560]{1,0:T(8,128)(2,1)}, u32[]{:S(2)}) copy-start(bf16[512,2560]{1,0:T(8,128)(2,1)} %param.15) | copy-start | bytes 7864324
  37.2 19.5 %copy-start.10 = (bf16[1280,160]{0,1:T(8,128)(2,1)S(1)}, bf16[1280,160]{0,1:T(8,128)(2,1)}, u32[]{:S(2)}) copy-start(bf16[1280,160]{0,1:T(8,128)(2,1)} %param.12) | copy-start | bytes 1228804
  38.3 18.4 %all-to-all-start.1 = ((bf16[16,80,384]{2,1,0:T(8,128)(2,1)}), bf16[16,80,384]{2,1,0:T(8,128)(2,1)}, u32[]{:S(2)}, u32[]{:S(2)}) async-start(bf16[16,80,384]{2,1,0:T(8,128)(2,1)} %broadcast_in_dim.85), calls=%async_computation.1 | async-start | bytes 1966080 | tf_op jit(solution)/shard_map/all_to_all | solution.py:35
  58.3 39.1 %copy-start.13 = (s32[8]{0:T(128)S(1)}, s32[8]{0:T(128)}, u32[]{:S(2)}) copy-start(s32[8]{0:T(128)} %param.17) | copy-start | bytes 100
  58.3 39.8 %copy-start.11 = (f32[2560]{0:T(1024)S(1)}, f32[2560]{0:T(1024)}, u32[]{:S(2)}) copy-start(f32[2560]{0:T(1024)} %param.16) | copy-start | bytes 30724
  58.3 4.4 %collective-permute-start = (f32[80,384]{1,0:T(8,128)S(1)}, f32[80,384]{1,0:T(8,128)S(1)}, u32[]{:S(2)}, u32[]{:S(2)}) collective-permute-start(f32[80,384]{1,0:T(8,128)S(1)} %dynamic-slice_bitcast_fusion), channel_id=1, source_target_pairs={{0,32},{32,0},{64,96},{96,64},{128,160},{160,128},{192,224},{224,1... | collective-permute-start | bytes 368648 | tf_op jit(solution)/shard_map/ppermute | solution.py:22
  62.7 9.3 %collective-permute-start.3 = (bf16[80,384]{1,0:T(8,128)(2,1)S(1)}, bf16[80,384]{1,0:T(8,128)(2,1)S(1)}, u32[]{:S(2)}, u32[]{:S(2)}) collective-permute-start(bf16[80,384]{1,0:T(8,128)(2,1)S(1)} %fusion.22), channel_id=1, source_target_pairs={{0,192},{32,224},{64,0},{96,32},{128,64},{160,96},{192,128},{224,1... | collective-permute-start | bytes 184328 | tf_op jit(solution)/shard_map/ppermute | solution.py:27
  68.8 7.2 %collective-permute-start.2 = (bf16[80,384]{1,0:T(8,128)(2,1)S(1)}, bf16[80,384]{1,0:T(8,128)(2,1)S(1)}, u32[]{:S(2)}, u32[]{:S(2)}) collective-permute-start(bf16[80,384]{1,0:T(8,128)(2,1)S(1)} %fusion.22), channel_id=1, source_target_pairs={{0,128},{32,160},{64,192},{96,224},{128,0},{160,32},{192,64},{224,... | collective-permute-start | bytes 184328 | tf_op jit(solution)/shard_map/ppermute | solution.py:27
  69.8 6.9 %collective-permute-start.1 = (bf16[80,384]{1,0:T(8,128)(2,1)S(1)}, bf16[80,384]{1,0:T(8,128)(2,1)S(1)}, u32[]{:S(2)}, u32[]{:S(2)}) collective-permute-start(bf16[80,384]{1,0:T(8,128)(2,1)S(1)} %fusion.22), channel_id=1, source_target_pairs={{0,64},{32,96},{64,128},{96,160},{128,192},{160,224},{192,0},{224,... | collective-permute-start | bytes 184328 | tf_op jit(solution)/shard_map/ppermute | solution.py:27
  94.3 8.9 %collective-permute-start.4 = (bf16[16,80,384]{2,1,0:T(8,128)(2,1)}, bf16[16,80,384]{2,1,0:T(8,128)(2,1)}, u32[]{:S(2)}, u32[]{:S(2)}) collective-permute-start(bf16[16,80,384]{2,1,0:T(8,128)(2,1)} %all_to_all.36), channel_id=1, source_target_pairs={{0,32},{32,0},{64,96},{96,64},{128,160},{160,128},{192,224},{224,1... | collective-permute-start | bytes 2949128 | tf_op jit(solution)/shard_map/ppermute | solution.py:22
  110.8 17.8 %all-to-all-start.4 = ((bf16[16,64,384]{2,1,0:T(8,128)(2,1)}), bf16[16,64,384]{2,1,0:T(8,128)(2,1)S(1)}, u32[]{:S(2)}, u32[]{:S(2)}) async-start(bf16[16,64,384]{2,1,0:T(8,128)(2,1)} %slice.48), calls=%async_computation.4 | async-start | bytes 1572864 | tf_op jit(solution)/shard_map/all_to_all | solution.py:35
  128.5 21.3 %all-to-all-start.3 = ((bf16[16,96,384]{2,1,0:T(8,128)(2,1)}), bf16[16,96,384]{2,1,0:T(8,128)(2,1)}, u32[]{:S(2)}, u32[]{:S(2)}) async-start(bf16[16,96,384]{2,1,0:T(8,128)(2,1)} %slice.47), calls=%async_computation.3 | async-start | bytes 2359296 | tf_op jit(solution)/shard_map/all_to_all | solution.py:35
  133.0 4.0 %copy-start.4 = (bf16[16,80,384]{2,1,0:T(8,128)(2,1)S(1)}, bf16[16,80,384]{2,1,0:T(8,128)(2,1)}, u32[]{:S(2)}) copy-start(bf16[16,80,384]{2,1,0:T(8,128)(2,1)} %copy-done.3) | copy-start | bytes 2949124
  139.0 34.0 %copy-start.7 = (f32[160,384]{1,0:T(8,128)S(1)}, f32[160,384]{1,0:T(8,128)}, u32[]{:S(2)}) copy-start(f32[160,384]{1,0:T(8,128)} %convert_subtract_fusion) | copy-start | bytes 737284
  190.1 18.7 %all-to-all-start.6 = ((bf16[16,72,384]{2,1,0:T(8,128)(2,1)}), bf16[16,72,384]{2,1,0:T(8,128)(2,1)S(1)}, u32[]{:S(2)}, u32[]{:S(2)}) async-start(bf16[16,72,384]{2,1,0:T(8,128)(2,1)} %broadcast_in_dim.97), calls=%async_computation.6 | async-start | bytes 1769472 | tf_op jit(solution)/shard_map/all_to_all | solution.py:35
  196.0 23.5 %collective-permute-start.5 = (bf16[16,80,384]{2,1,0:T(8,128)(2,1)}, bf16[16,80,384]{2,1,0:T(8,128)(2,1)}, u32[]{:S(2)}, u32[]{:S(2)}) collective-permute-start(bf16[16,80,384]{2,1,0:T(8,128)(2,1)} %pad_maximum_fusion.2), channel_id=1, source_target_pairs={{0,1},{1,0},{2,3},{3,2},{4,5},{5,4},{6,7},{7,6},{8,9},{9,8},{10,11... | collective-permute-start | bytes 2949128 | tf_op jit(solution)/shard_map/ppermute | solution.py:31
  210.7 21.1 %all-to-all-start.5 = ((bf16[16,96,384]{2,1,0:T(8,128)(2,1)}), bf16[16,96,384]{2,1,0:T(8,128)(2,1)}, u32[]{:S(2)}, u32[]{:S(2)}) async-start(bf16[16,96,384]{2,1,0:T(8,128)(2,1)} %broadcast_in_dim.90), calls=%async_computation.5 | async-start | bytes 2359296 | tf_op jit(solution)/shard_map/all_to_all | solution.py:35
  215.1 41.2 %collective-permute-start.7 = (bf16[512,384]{1,0:T(8,128)(2,1)}, bf16[512,384]{1,0:T(8,128)(2,1)}, u32[]{:S(2)}, u32[]{:S(2)}) collective-permute-start(bf16[512,384]{1,0:T(8,128)(2,1)} %copy-done.8), channel_id=1, source_target_pairs={{0,1},{1,0},{2,3},{3,2},{4,5},{5,4},{6,7},{7,6},{8,9},{9,8},{10,11... | collective-permute-start | bytes 1179656 | tf_op jit(solution)/shard_map/ppermute | solution.py:31
  223.3 4.6 %collective-permute-start.10 = (f32[8,128]{1,0:T(8,128)S(1)}, f32[8,128]{1,0:T(8,128)S(1)}, u32[]{:S(2)}, u32[]{:S(2)}) collective-permute-start(f32[8,128]{1,0:T(8,128)S(1)} %broadcast_in_dim.98), channel_id=1, source_target_pairs={{0,1},{1,0},{2,3},{3,2},{4,5},{5,4},{6,7},{7,6},{8,9},{9,8},{10,11... | collective-permute-start | bytes 12296 | tf_op jit(solution)/shard_map/ppermute | solution.py:31
  224.5 20.5 %collective-permute-start.9 = (bf16[8,64,384]{2,1,0:T(8,128)(2,1)}, bf16[8,64,384]{2,1,0:T(8,128)(2,1)}, u32[]{:S(2)}, u32[]{:S(2)}) collective-permute-start(bf16[8,64,384]{2,1,0:T(8,128)(2,1)} %constant_dynamic-slice_fusion), channel_id=1, source_target_pairs={{0,1},{1,0},{2,3},{3,2},{4,5},{5,4},{6,7},{7,6},{8,9},{9,8},{10,11... | collective-permute-start | bytes 1179656 | tf_op jit(solution)/shard_map/ppermute | solution.py:31
  229.8 3.8 %copy-start.14 = (f32[512,384]{1,0:T(8,128)S(1)}, f32[512,384]{1,0:T(8,128)}, u32[]{:S(2)}) copy-start(f32[512,384]{1,0:T(8,128)} %get-tuple-element.30) | copy-start | bytes 2359300
  233.6 4.4 %copy-start.5 = (bf16[8,160,384]{2,1,0:T(8,128)(2,1)S(1)}, bf16[8,160,384]{2,1,0:T(8,128)(2,1)}, u32[]{:S(2)}) copy-start(bf16[8,160,384]{2,1,0:T(8,128)(2,1)} %maximum_select_fusion) | copy-start | bytes 2949124
  235.1 7.5 %collective-permute-start.6 = (bf16[512,384]{1,0:T(8,128)(2,1)S(1)}, bf16[512,384]{1,0:T(8,128)(2,1)S(1)}, u32[]{:S(2)}, u32[]{:S(2)}) collective-permute-start(bf16[512,384]{1,0:T(8,128)(2,1)S(1)} %fusion.3), channel_id=1, source_target_pairs={{0,1},{1,0},{2,3},{3,2},{4,5},{5,4},{6,7},{7,6},{8,9},{9,8},{10,11... | collective-permute-start | bytes 1179656 | tf_op jit(solution)/shard_map/ppermute | solution.py:31
  236.4 18.8 %collective-permute-start.8 = (bf16[8,96,384]{2,1,0:T(8,128)(2,1)S(1)}, bf16[8,96,384]{2,1,0:T(8,128)(2,1)S(1)}, u32[]{:S(2)}, u32[]{:S(2)}) collective-permute-start(bf16[8,96,384]{2,1,0:T(8,128)(2,1)S(1)} %constant_dynamic-slice_fusion.1), channel_id=1, source_target_pairs={{0,1},{1,0},{2,3},{3,2},{4,5},{5,4},{6,7},{7,6},{8,9},{9,8},{10,11... | collective-permute-start | bytes 1769480 | tf_op jit(solution)/shard_map/ppermute | solution.py:31
  (7 other events, 13.8 us)

commit v3 on v2

--- a/solution.py
+++ b/solution.py
@@ -60,7 +60,7 @@
     tok_index = lax.axis_index("tok")
     core = segment_index % 2
     shards = lax.axis_size("shard")
-    tokens, width_slice = activations.shape
+    tokens, _ = activations.shape
     tokens_all = tokens * lax.axis_size("tok")
     width = decoder_bias.shape[0]
     half = width // 2
@@ -105,11 +105,6 @@
     def tok_half(pieces, which):
         return lax.dynamic_slice_in_dim(pieces, which * (shards // 2), shards // 2, 0)
 
-    target = by_core(
-        lax.dynamic_index_in_dim(mine, shard_index, 0, keepdims=False),
-        lax.dynamic_index_in_dim(other, shard_index, 0, keepdims=False),
-        0,
-    ).astype(F32)
     sent = [tok_half(c, 1 - tok_index) for c in (centered_mine, centered_other)]
     centered_peer = tok_swap(jnp.concatenate(sent, axis=0))
 
@@ -124,12 +119,33 @@
     slope = jnp.where(live_mask, jax.nn.sigmoid(10.0 * pre_act), 0.0)
     codes_other = tok_swap(codes)
 
-    part = dot(decoder_weight, codes, 0, 0).astype(BF16)
-    split = 96
-    part = with_layout_constraint(part, Layout((0, 1))).reshape(shards, width_slice, tokens)
-    start = shard_index * width_slice
-    bias_slice = lax.dynamic_slice_in_dim(decoder_bias, start, width_slice, 0)[:, None]
-    base = bias_slice - target
+    count = shards // 2
+    cut = 3 * half // 5
+    rows_a, rows_b = cut // count, (half - cut) // count
+
+    def columns_of(low, high):
+        return lax.optimization_barrier(
+            jnp.concatenate(
+                [decoder_weight[:, low:high], decoder_weight[:, half + low : half + high]], axis=1
+            )
+        )
+
+    decoder_a = columns_of(0, cut)
+    decoder_b = columns_of(cut, half)
+    mlp_full = lax.optimization_barrier(by_core(mine, other, 1).reshape(width, tokens))
+    half_start = (shard_index // count) * half
+
+    def base_of(offset, size):
+        start = half_start + offset + (shard_index % count) * size
+        bias = lax.dynamic_slice_in_dim(decoder_bias, start, size, 0)[:, None]
+        return bias - lax.dynamic_slice_in_dim(mlp_full, start, size, 0).astype(F32)
+
+    base_a, base_b = base_of(0, rows_a), base_of(cut, rows_b)
+
+    def part_of(columns, size):
+        part = with_layout_constraint(dot(columns, codes, 0, 0).astype(BF16), Layout((0, 1)))
+        return part.reshape(shards, size, tokens)
+
     places = jnp.arange(segment_total)
     up_to = (places <= segment_index).astype(F32)[:, None, None]
     weight = (segment_total - jnp.maximum(places, segment_index)).astype(F32)[:, None, None]
@@ -142,14 +158,14 @@
         summed = base_weight * base + jnp.sum(parts * weight, axis=0)
         return (summed * scale).astype(BF16), jnp.sum(errors * errors, axis=0, keepdims=True)
 
-    sum_first = shard_sum(part[:, :split]).astype(BF16)
-    sum_second = shard_sum(part[:, split:]).astype(BF16)
-    slice_first, square_first = seg_step(sum_first, base[:split])
+    sum_first = shard_sum(part_of(decoder_a, rows_a)).astype(BF16)
+    sum_second = shard_sum(part_of(decoder_b, rows_b)).astype(BF16)
+    slice_first, square_first = seg_step(sum_first, base_a)
     slice_first, square_first, sum_second = lax.optimization_barrier(
         (slice_first, square_first, sum_second)
     )
     back_first = shard_gather(slice_first)
-    slice_second, square_second = seg_step(sum_second, base[split:])
+    slice_second, square_second = seg_step(sum_second, base_b)
 
     square = square_first + square_second
     high = square.astype(BF16)
@@ -158,32 +174,32 @@
     extra = jnp.where(row == 0, high, jnp.where(row == 1, low, jnp.zeros_like(low)))
     back_second = shard_gather(jnp.concatenate([slice_second, extra], axis=0))
 
-    def joined(first, second):
-        return jnp.concatenate([first, second], axis=1).reshape(-1, tokens)
-
     first_other = tok_swap(tok_half(back_first, 1 - tok_index))
-    rest = width_slice - split
     second_other = tok_swap(
         lax.dynamic_slice(
-            back_second,
-            ((1 - tok_index) * (shards // 2), 0, 0),
-            (shards // 2, rest, tokens),
+            back_second, ((1 - tok_index) * count, 0, 0), (count, rows_b, tokens)
         )
     )
-    back = joined(back_first, back_second[:, :rest])
-    code_acc = dot(decoder_weight, back, 1, 0)
-    code_grad = (code_acc * slope).astype(BF16)
+    acc_first = dot(decoder_a, back_first.reshape(-1, tokens), 1, 0)
+    acc_first = lax.optimization_barrier(acc_first)
+    acc_second = dot(decoder_b, back_second[:, :rows_b].reshape(-1, tokens), 1, 0)
+    code_grad = ((acc_first + acc_second) * slope).astype(BF16)
     code_grad_other = tok_swap(code_grad)
 
-    squares = jnp.broadcast_to(jnp.sum(back_second[:, rest:].astype(F32)), (8, 128))
+    squares = jnp.broadcast_to(jnp.sum(back_second[:, rows_b:].astype(F32)), (8, 128))
     squares = squares + tok_swap(squares)
     prefix_mse = squares[0, :1] / (tokens_all * width)
 
-    back_mine = lax.dynamic_slice_in_dim(back, tok_index * half, half, 0)
+    def joined(first, second):
+        return jnp.concatenate([first.reshape(-1, tokens), second.reshape(-1, tokens)], axis=0)
+
+    back_mine = joined(
+        tok_half(back_first, tok_index),
+        lax.dynamic_slice(back_second, (tok_index * count, 0, 0), (count, rows_b, tokens)),
+    )
     back_other = joined(first_other, second_other)
     grad_decoder = dot(codes, back_mine, 1, 1)
     grad_decoder = grad_decoder + dot(codes_other, back_other, 1, 1)
-    count = shards // 2
     own = by_core(tok_half(centered_mine, tok_index), tok_half(centered_other, tok_index), 1)
     own = lax.optimization_barrier(own.reshape(half, tokens))
     peer = by_core(centered_peer[:count], centered_peer[count:], 1)

time: 264 us -> 260 us (0.985)
  blocking collectives: 86.6 us -> 69.7 us
  waiting for transfers between devices: 73 us -> 84.7 us
  other arithmetic: 18.8 us -> 15.1 us
    all_to_all x2 -> x1, blocking collectives: 50.2 us -> 32.7 us  [shard_exchange(): return lax.all_to_all(pieces, 'shard', 0, 0)]
    all_to_all x5 -> x6, waiting for transfers between devices: 51.5 us -> 58.7 us  [shard_exchange(): return lax.all_to_all(pieces, 'shard', 0, 0)]
    ppermute x6, waiting for transfers between devices: 15.9 us -> 20.4 us  [tok_swap(): return lax.ppermute(value, 'tok', [(0, 1), (1, 0)])]
    unnamed x30 -> x64, local copies, waits for them, and re-layouts: 1.41 us -> 4.81 us
    dynamic_slice x2 -> x3, local copies, waits for them, and re-layouts: 0.88 us -> 3.61 us  [the longest x2 2.6 us: base_of(): bias = lax.dynamic_slice_in_dim(decoder_bias, start, size, 0)[:, None]]
    dot_general x11 -> x13, matrix products: 18.6 us -> 21.1 us  [dot(): lax.dot_general(left, right, (((left_dim,), (right_dim,)), ((), ())), pre...]
    all_to_all x5 -> x6, starting transfers between devices: 20.3 us -> 22.7 us  [shard_exchange(): return lax.all_to_all(pieces, 'shard', 0, 0)]
  transfers between devices with their start and end apart: 16 -> 17, of which waited for: 12 -> 13; matrix products, arithmetic and copies ran while one was open for 14% -> 14% of each run, Pallas kernels for 0% -> 0%
where the time goes in v3:
time: 260 us; the launch traced here: 257 us
  waiting for transfers between devices  84.7 us (33%)
  blocking collectives  69.7 us (27%)
  starting transfers between devices  41.4 us (16%)
  local copies, waits for them, and re-layouts  22 us (8%)
  matrix products  21.1 us (8%)
  other arithmetic  15.1 us (6%)
  between operations  3.01 us (1%)
    all_to_all x6, waiting for transfers between devices, shard_exchange(): return lax.all_to_all(pieces, 'shard', 0, 0)  58.7 us
    all_gather x2, blocking collectives, seg_step(): parts = lax.all_gather(mine, 'seg').astype(F32)  37 us
    all_to_all x1, blocking collectives, shard_exchange(): return lax.all_to_all(pieces, 'shard', 0, 0)  32.7 us
    all_to_all x6, starting transfers between devices, shard_exchange(): return lax.all_to_all(pieces, 'shard', 0, 0)  22.7 us
    dot_general x13, matrix products, dot(): lax.dot_general(left, right, (((left_dim,), (right_dim,)), ((), ())), pre...  21.1 us
    ppermute x6, waiting for transfers between devices, tok_swap(): return lax.ppermute(value, 'tok', [(0, 1), (1, 0)])  20.4 us
    ppermute x3, starting transfers between devices, chip_shift(): lax.ppermute(value, 'seg', [(i, (i + 2 * step) % count) for i in range(co...  9.34 us
    ppermute x2, starting transfers between devices, core_swap(): return lax.ppermute(value, 'seg', [(i, i ^ 1) for i in range(count)])  6.3 us
  transfers between devices with their start and end apart: 17, of which 13 were waited for; matrix products, arithmetic and copies ran while one was open for 14% of the time, Pallas kernels for 0%

profile of v3, /device:TPU:1, one launch (start us, length us, event | category | flops | bytes accessed | tf_op | source)
XLA Modules:
  0.0 257.0 jit_solution(12471687471784931037)
XLA Ops:
  4.9 32.7 %all_to_all.35 = bf16[16,160,384]{2,1,0:T(8,128)(2,1)S(1)} all-to-all(bf16[16,160,384]{2,1,0:T(8,128)(2,1)S(1)} %pad_maximum_fusion), channel_id=1, replica_groups=mesh['seg'=8,'shard'=16,'tok'=2] {'shard'}, dimensions={0} | all-to-all | bytes 3932160 | tf_op jit(solution)/shard_map/all_to_all | solution.py:35
  39.0 4.3 %all-to-all-start.1 = ((bf16[16,80,384]{2,1,0:T(8,128)(2,1)}), bf16[16,80,384]{2,1,0:T(8,128)(2,1)S(1)}, u32[]{:S(2)}, u32[]{:S(2)}) async-start(bf16[16,80,384]{2,1,0:T(8,128)(2,1)} %broadcast_in_dim.86), calls=%async_computation.1 | async-start | bytes 1966080 | tf_op jit(solution)/shard_map/all_to_all | solution.py:35
  43.3 14.4 %all-to-all-done.1 = bf16[16,80,384]{2,1,0:T(8,128)(2,1)S(1)} async-done(((bf16[16,80,384]{2,1,0:T(8,128)(2,1)}), bf16[16,80,384]{2,1,0:T(8,128)(2,1)S(1)}, u32[]{:S(2)}, u32[]{:S(2)}) %all-to-all-start.1) | async-done | bytes 983072 | tf_op jit(solution)/shard_map/all_to_all | solution.py:35
  58.0 3.1 %collective-permute-start = (f32[80,384]{1,0:T(8,128)S(1)}, f32[80,384]{1,0:T(8,128)S(1)}, u32[]{:S(2)}, u32[]{:S(2)}) collective-permute-start(f32[80,384]{1,0:T(8,128)S(1)} %dynamic-slice_bitcast_fusion), channel_id=1, source_target_pairs={{0,32},{32,0},{64,96},{96,64},{128,160},{160,128},{192,224},{224,1... | collective-permute-start | bytes 368648 | tf_op jit(solution)/shard_map/ppermute | solution.py:22
  62.1 6.1 %collective-permute-start.3 = (bf16[80,384]{1,0:T(8,128)(2,1)S(1)}, bf16[80,384]{1,0:T(8,128)(2,1)S(1)}, u32[]{:S(2)}, u32[]{:S(2)}) collective-permute-start(bf16[80,384]{1,0:T(8,128)(2,1)S(1)} %fusion.27), channel_id=1, source_target_pairs={{0,192},{32,224},{64,0},{96,32},{128,64},{160,96},{192,128},{224,1... | collective-permute-start | bytes 184328 | tf_op jit(solution)/shard_map/ppermute | solution.py:27
  71.5 3.9 %collective-permute-done.2 = bf16[80,384]{1,0:T(8,128)(2,1)S(1)} collective-permute-done((bf16[80,384]{1,0:T(8,128)(2,1)S(1)}, bf16[80,384]{1,0:T(8,128)(2,1)S(1)}, u32[]{:S(2)}, u32[]{:S(2)}) %collective-permute-start.2) | collective-permute-done | bytes 61472 | tf_op jit(solution)/shard_map/ppermute | solution.py:27
  77.1 3.6 %all-to-all-start.2 = ((bf16[16,80,384]{2,1,0:T(8,128)(2,1)}), bf16[16,80,384]{2,1,0:T(8,128)(2,1)S(1)}, u32[]{:S(2)}, u32[]{:S(2)}) async-start(bf16[16,80,384]{2,1,0:T(8,128)(2,1)} %broadcast_in_dim.87), calls=%async_computation.2 | async-start | bytes 1966080 | tf_op jit(solution)/shard_map/all_to_all | solution.py:35
  83.3 11.6 %all-to-all-done.2 = bf16[16,80,384]{2,1,0:T(8,128)(2,1)S(1)} async-done(((bf16[16,80,384]{2,1,0:T(8,128)(2,1)}), bf16[16,80,384]{2,1,0:T(8,128)(2,1)S(1)}, u32[]{:S(2)}, u32[]{:S(2)}) %all-to-all-start.2) | async-done | bytes 983072 | tf_op jit(solution)/shard_map/all_to_all | solution.py:35
  94.9 3.2 %collective-permute-start.4 = (bf16[16,80,384]{2,1,0:T(8,128)(2,1)S(1)}, bf16[16,80,384]{2,1,0:T(8,128)(2,1)S(1)}, u32[]{:S(2)}, u32[]{:S(2)}) collective-permute-start(bf16[16,80,384]{2,1,0:T(8,128)(2,1)S(1)} %all-to-all-done.2), channel_id=1, source_target_pairs={{0,32},{32,0},{64,96},{96,64},{128,160},{160,128},{192,224},{224,1... | collective-permute-start | bytes 2949128 | tf_op jit(solution)/shard_map/ppermute | solution.py:22
  108.9 3.6 %all-to-all-start.4 = ((bf16[16,64,384]{2,1,0:T(8,128)(2,1)}), bf16[16,64,384]{2,1,0:T(8,128)(2,1)S(1)}, u32[]{:S(2)}, u32[]{:S(2)}) async-start(bf16[16,64,384]{2,1,0:T(8,128)(2,1)} %bitcast.83), calls=%async_computation.4 | async-start | bytes 1572864 | tf_op jit(solution)/shard_map/all_to_all | solution.py:35
  117.3 9.2 %all-to-all-done.4 = bf16[16,64,384]{2,1,0:T(8,128)(2,1)S(1)} async-done(((bf16[16,64,384]{2,1,0:T(8,128)(2,1)}), bf16[16,64,384]{2,1,0:T(8,128)(2,1)S(1)}, u32[]{:S(2)}, u32[]{:S(2)}) %all-to-all-start.4) | async-done | bytes 786464 | tf_op jit(solution)/shard_map/all_to_all | solution.py:35
  127.4 3.9 %all-to-all-start.3 = ((bf16[16,96,384]{2,1,0:T(8,128)(2,1)}), bf16[16,96,384]{2,1,0:T(8,128)(2,1)S(1)}, u32[]{:S(2)}, u32[]{:S(2)}) async-start(bf16[16,96,384]{2,1,0:T(8,128)(2,1)} %bitcast.82), calls=%async_computation.3 | async-start | bytes 2359296 | tf_op jit(solution)/shard_map/all_to_all | solution.py:35
  140.0 7.9 %all-to-all-done.3 = bf16[16,96,384]{2,1,0:T(8,128)(2,1)S(1)} async-done(((bf16[16,96,384]{2,1,0:T(8,128)(2,1)}), bf16[16,96,384]{2,1,0:T(8,128)(2,1)S(1)}, u32[]{:S(2)}, u32[]{:S(2)}) %all-to-all-start.3) | async-done | bytes 1179680 | tf_op jit(solution)/shard_map/all_to_all | solution.py:35
  148.1 21.9 %all-gather = bf16[768,384]{1,0:T(8,128)(2,1)S(1)} all-gather(bf16[96,384]{1,0:T(8,128)(2,1)S(1)} %reduce_sum.107), channel_id=2, replica_groups=mesh['seg'=8,'shard'=16,'tok'=2] {'seg'}, dimensions={0}, use_global_device_ids=true | all-gather | bytes 663552 | tf_op jit(solution)/shard_map/all_gather | solution.py:156
  171.4 15.0 %all-gather.1 = bf16[512,384]{1,0:T(8,128)(2,1)S(1)} all-gather(bf16[64,384]{1,0:T(8,128)(2,1)S(1)} %reduce_sum.111), channel_id=3, replica_groups=mesh['seg'=8,'shard'=16,'tok'=2] {'seg'}, dimensions={0}, use_global_device_ids=true | all-gather | bytes 442368 | tf_op jit(solution)/shard_map/all_gather | solution.py:156
  188.7 3.6 %all-to-all-start.6 = ((bf16[16,72,384]{2,1,0:T(8,128)(2,1)}), bf16[16,72,384]{2,1,0:T(8,128)(2,1)S(1)}, u32[]{:S(2)}, u32[]{:S(2)}) async-start(bf16[16,72,384]{2,1,0:T(8,128)(2,1)} %broadcast_in_dim.98), calls=%async_computation.6 | async-start | bytes 1769472 | tf_op jit(solution)/shard_map/all_to_all | solution.py:35
  193.5 13.9 %all-to-all-done.6 = bf16[16,72,384]{2,1,0:T(8,128)(2,1)S(1)} async-done(((bf16[16,72,384]{2,1,0:T(8,128)(2,1)}), bf16[16,72,384]{2,1,0:T(8,128)(2,1)S(1)}, u32[]{:S(2)}, u32[]{:S(2)}) %all-to-all-start.6) | async-done | bytes 884768 | tf_op jit(solution)/shard_map/all_to_all | solution.py:35
  208.6 3.7 %all-to-all-start.5 = ((bf16[16,96,384]{2,1,0:T(8,128)(2,1)}), bf16[16,96,384]{2,1,0:T(8,128)(2,1)S(1)}, u32[]{:S(2)}, u32[]{:S(2)}) async-start(bf16[16,96,384]{2,1,0:T(8,128)(2,1)} %broadcast_in_dim.91), calls=%async_computation.5 | async-start | bytes 2359296 | tf_op jit(solution)/shard_map/all_to_all | solution.py:35
  213.7 3.3 %collective-permute-done.5 = bf16[16,80,384]{2,1,0:T(8,128)(2,1)} collective-permute-done((bf16[16,80,384]{2,1,0:T(8,128)(2,1)}, bf16[16,80,384]{2,1,0:T(8,128)(2,1)}, u32[]{:S(2)}, u32[]{:S(2)}) %collective-permute-start.5) | collective-permute-done | bytes 983072 | tf_op jit(solution)/shard_map/ppermute | solution.py:31
  222.5 3.0 %collective-permute-done.10 = f32[8,128]{1,0:T(8,128)S(1)} collective-permute-done((f32[8,128]{1,0:T(8,128)S(1)}, f32[8,128]{1,0:T(8,128)S(1)}, u32[]{:S(2)}, u32[]{:S(2)}) %collective-permute-start.10) | collective-permute-done | bytes 4128 | tf_op jit(solution)/shard_map/ppermute | solution.py:31
  229.0 2.5 fusion.35
  235.9 3.9 %collective-permute-done.6 = bf16[512,384]{1,0:T(8,128)(2,1)S(1)} collective-permute-done((bf16[512,384]{1,0:T(8,128)(2,1)S(1)}, bf16[512,384]{1,0:T(8,128)(2,1)S(1)}, u32[]{:S(2)}, u32[]{:S(2)}) %collective-permute-start.6) | collective-permute-done | bytes 393248 | tf_op jit(solution)/shard_map/ppermute | solution.py:31
  242.2 10.2 %collective-permute-done.8 = bf16[8,96,384]{2,1,0:T(8,128)(2,1)S(1)} collective-permute-done((bf16[8,96,384]{2,1,0:T(8,128)(2,1)S(1)}, bf16[8,96,384]{2,1,0:T(8,128)(2,1)S(1)}, u32[]{:S(2)}, u32[]{:S(2)}) %collective-permute-start.8) | collective-permute-done | bytes 589856 | tf_op jit(solution)/shard_map/ppermute | solution.py:31
  252.4 3.5 %convolution_add_fusion = f32[512,1280]{1,0:T(8,128)} fusion(f32[512,1280]{1,0:T(8,128)S(1)} %fusion.6, bf16[512,384]{1,0:T(8,128)(2,1)} %collective-permute-done.7, bf16[512,384]{1,0:T(8,128)(2,1)} %bitcast.29, bf16[768,384]{1,0:T(8,128)(2,1)S(1)} %bitcast.84), kind=kOutput, calls=%fused_computation.1 | convolution fusion | flops 505937920 | bytes 6619136 | tf_op jit(solution)/shard_map/dot_general | solution.py:15
  (141 shorter events, 61.8 us)
Async XLA Ops:
  37.9 19.8 %copy-start.16 = (bf16[1280,160]{0,1:T(8,128)(2,1)S(1)}, bf16[1280,160]{0,1:T(8,128)(2,1)}, u32[]{:S(2)}) copy-start(bf16[1280,160]{0,1:T(8,128)(2,1)} %param.12) | copy-start | bytes 1228804
  39.0 18.6 %all-to-all-start.1 = ((bf16[16,80,384]{2,1,0:T(8,128)(2,1)}), bf16[16,80,384]{2,1,0:T(8,128)(2,1)S(1)}, u32[]{:S(2)}, u32[]{:S(2)}) async-start(bf16[16,80,384]{2,1,0:T(8,128)(2,1)} %broadcast_in_dim.86), calls=%async_computation.1 | async-start | bytes 1966080 | tf_op jit(solution)/shard_map/all_to_all | solution.py:35
  58.0 4.1 %collective-permute-start = (f32[80,384]{1,0:T(8,128)S(1)}, f32[80,384]{1,0:T(8,128)S(1)}, u32[]{:S(2)}, u32[]{:S(2)}) collective-permute-start(f32[80,384]{1,0:T(8,128)S(1)} %dynamic-slice_bitcast_fusion), channel_id=1, source_target_pairs={{0,32},{32,0},{64,96},{96,64},{128,160},{160,128},{192,224},{224,1... | collective-permute-start | bytes 368648 | tf_op jit(solution)/shard_map/ppermute | solution.py:22
  62.1 9.3 %collective-permute-start.3 = (bf16[80,384]{1,0:T(8,128)(2,1)S(1)}, bf16[80,384]{1,0:T(8,128)(2,1)S(1)}, u32[]{:S(2)}, u32[]{:S(2)}) collective-permute-start(bf16[80,384]{1,0:T(8,128)(2,1)S(1)} %fusion.27), channel_id=1, source_target_pairs={{0,192},{32,224},{64,0},{96,32},{128,64},{160,96},{192,128},{224,1... | collective-permute-start | bytes 184328 | tf_op jit(solution)/shard_map/ppermute | solution.py:27
  68.2 7.2 %collective-permute-start.2 = (bf16[80,384]{1,0:T(8,128)(2,1)S(1)}, bf16[80,384]{1,0:T(8,128)(2,1)S(1)}, u32[]{:S(2)}, u32[]{:S(2)}) collective-permute-start(bf16[80,384]{1,0:T(8,128)(2,1)S(1)} %fusion.27), channel_id=1, source_target_pairs={{0,128},{32,160},{64,192},{96,224},{128,0},{160,32},{192,64},{224,... | collective-permute-start | bytes 184328 | tf_op jit(solution)/shard_map/ppermute | solution.py:27
  69.2 6.9 %collective-permute-start.1 = (bf16[80,384]{1,0:T(8,128)(2,1)S(1)}, bf16[80,384]{1,0:T(8,128)(2,1)S(1)}, u32[]{:S(2)}, u32[]{:S(2)}) collective-permute-start(bf16[80,384]{1,0:T(8,128)(2,1)S(1)} %fusion.27), channel_id=1, source_target_pairs={{0,64},{32,96},{64,128},{96,160},{128,192},{160,224},{192,0},{224,... | collective-permute-start | bytes 184328 | tf_op jit(solution)/shard_map/ppermute | solution.py:27
  77.1 17.8 %all-to-all-start.2 = ((bf16[16,80,384]{2,1,0:T(8,128)(2,1)}), bf16[16,80,384]{2,1,0:T(8,128)(2,1)S(1)}, u32[]{:S(2)}, u32[]{:S(2)}) async-start(bf16[16,80,384]{2,1,0:T(8,128)(2,1)} %broadcast_in_dim.87), calls=%async_computation.2 | async-start | bytes 1966080 | tf_op jit(solution)/shard_map/all_to_all | solution.py:35
  94.9 7.7 %collective-permute-start.4 = (bf16[16,80,384]{2,1,0:T(8,128)(2,1)S(1)}, bf16[16,80,384]{2,1,0:T(8,128)(2,1)S(1)}, u32[]{:S(2)}, u32[]{:S(2)}) collective-permute-start(bf16[16,80,384]{2,1,0:T(8,128)(2,1)S(1)} %all-to-all-done.2), channel_id=1, source_target_pairs={{0,32},{32,0},{64,96},{96,64},{128,160},{160,128},{192,224},{224,1... | collective-permute-start | bytes 2949128 | tf_op jit(solution)/shard_map/ppermute | solution.py:22
  108.9 17.6 %all-to-all-start.4 = ((bf16[16,64,384]{2,1,0:T(8,128)(2,1)}), bf16[16,64,384]{2,1,0:T(8,128)(2,1)S(1)}, u32[]{:S(2)}, u32[]{:S(2)}) async-start(bf16[16,64,384]{2,1,0:T(8,128)(2,1)} %bitcast.83), calls=%async_computation.4 | async-start | bytes 1572864 | tf_op jit(solution)/shard_map/all_to_all | solution.py:35
  127.4 20.5 %all-to-all-start.3 = ((bf16[16,96,384]{2,1,0:T(8,128)(2,1)}), bf16[16,96,384]{2,1,0:T(8,128)(2,1)S(1)}, u32[]{:S(2)}, u32[]{:S(2)}) async-start(bf16[16,96,384]{2,1,0:T(8,128)(2,1)} %bitcast.82), calls=%async_computation.3 | async-start | bytes 2359296 | tf_op jit(solution)/shard_map/all_to_all | solution.py:35
  138.6 31.5 %copy-start.21 = (f32[8]{0:T(128)S(1)}, f32[8]{0:T(128)}, u32[]{:S(2)}) copy-start(f32[8]{0:T(128)} %compare_convert_fusion) | copy-start | bytes 100
  138.6 31.5 %copy-start.22 = (f32[8]{0:T(128)S(1)}, f32[8]{0:T(128)}, u32[]{:S(2)}) copy-start(f32[8]{0:T(128)} %subtract_convert_fusion.2) | copy-start | bytes 100
  139.9 30.5 %copy-start.26 = (f32[96]{0:T(128)S(1)}, f32[96]{0:T(128)}, u32[]{:S(2)}) copy-start(f32[96]{0:T(128)} %dynamic_slice.63) | copy-start | bytes 1156
  140.0 46.7 %copy-start.23 = (f32[64]{0:T(128)S(1)}, f32[64]{0:T(128)}, u32[]{:S(2)}) copy-start(f32[64]{0:T(128)} %dynamic_slice.67) | copy-start | bytes 772
  148.1 39.5 %copy-start.24 = (pred[8]{0:T(512)(128)(4,1)S(1)}, pred[8]{0:T(512)(128)(4,1)}, u32[]{:S(2)}) copy-start(pred[8]{0:T(512)(128)(4,1)} %get-tuple-element.39) | copy-start | bytes 28
  148.1 39.5 %copy-start.25 = (pred[8]{0:T(512)(128)(4,1)S(1)}, pred[8]{0:T(512)(128)(4,1)}, u32[]{:S(2)}) copy-start(pred[8]{0:T(512)(128)(4,1)} %get-tuple-element.40) | copy-start | bytes 28
  188.7 18.7 %all-to-all-start.6 = ((bf16[16,72,384]{2,1,0:T(8,128)(2,1)}), bf16[16,72,384]{2,1,0:T(8,128)(2,1)S(1)}, u32[]{:S(2)}, u32[]{:S(2)}) async-start(bf16[16,72,384]{2,1,0:T(8,128)(2,1)} %broadcast_in_dim.98), calls=%async_computation.6 | async-start | bytes 1769472 | tf_op jit(solution)/shard_map/all_to_all | solution.py:35
  193.5 23.5 %collective-permute-start.5 = (bf16[16,80,384]{2,1,0:T(8,128)(2,1)}, bf16[16,80,384]{2,1,0:T(8,128)(2,1)}, u32[]{:S(2)}, u32[]{:S(2)}) collective-permute-start(bf16[16,80,384]{2,1,0:T(8,128)(2,1)} %pad_maximum_fusion.3), channel_id=1, source_target_pairs={{0,1},{1,0},{2,3},{3,2},{4,5},{5,4},{6,7},{7,6},{8,9},{9,8},{10,11... | collective-permute-start | bytes 2949128 | tf_op jit(solution)/shard_map/ppermute | solution.py:31
  208.6 20.3 %all-to-all-start.5 = ((bf16[16,96,384]{2,1,0:T(8,128)(2,1)}), bf16[16,96,384]{2,1,0:T(8,128)(2,1)S(1)}, u32[]{:S(2)}, u32[]{:S(2)}) async-start(bf16[16,96,384]{2,1,0:T(8,128)(2,1)} %broadcast_in_dim.91), calls=%async_computation.5 | async-start | bytes 2359296 | tf_op jit(solution)/shard_map/all_to_all | solution.py:35
  212.3 29.8 %collective-permute-start.7 = (bf16[512,384]{1,0:T(8,128)(2,1)}, bf16[512,384]{1,0:T(8,128)(2,1)}, u32[]{:S(2)}, u32[]{:S(2)}) collective-permute-start(bf16[512,384]{1,0:T(8,128)(2,1)} %copy-done.17), channel_id=1, source_target_pairs={{0,1},{1,0},{2,3},{3,2},{4,5},{5,4},{6,7},{7,6},{8,9},{9,8},{10,11... | collective-permute-start | bytes 1179656 | tf_op jit(solution)/shard_map/ppermute | solution.py:31
  219.9 5.6 %collective-permute-start.10 = (f32[8,128]{1,0:T(8,128)S(1)}, f32[8,128]{1,0:T(8,128)S(1)}, u32[]{:S(2)}, u32[]{:S(2)}) collective-permute-start(f32[8,128]{1,0:T(8,128)S(1)} %broadcast_in_dim.99), channel_id=1, source_target_pairs={{0,1},{1,0},{2,3},{3,2},{4,5},{5,4},{6,7},{7,6},{8,9},{9,8},{10,11... | collective-permute-start | bytes 12296 | tf_op jit(solution)/shard_map/ppermute | solution.py:31
  221.3 20.9 %collective-permute-start.9 = (bf16[8,64,384]{2,1,0:T(8,128)(2,1)}, bf16[8,64,384]{2,1,0:T(8,128)(2,1)}, u32[]{:S(2)}, u32[]{:S(2)}) collective-permute-start(bf16[8,64,384]{2,1,0:T(8,128)(2,1)} %get-tuple-element.33), channel_id=1, source_target_pairs={{0,1},{1,0},{2,3},{3,2},{4,5},{5,4},{6,7},{7,6},{8,9},{9,8},{10,11... | collective-permute-start | bytes 1179656 | tf_op jit(solution)/shard_map/ppermute | solution.py:31
  232.3 7.4 %collective-permute-start.6 = (bf16[512,384]{1,0:T(8,128)(2,1)S(1)}, bf16[512,384]{1,0:T(8,128)(2,1)S(1)}, u32[]{:S(2)}, u32[]{:S(2)}) collective-permute-start(bf16[512,384]{1,0:T(8,128)(2,1)S(1)} %fusion.3), channel_id=1, source_target_pairs={{0,1},{1,0},{2,3},{3,2},{4,5},{5,4},{6,7},{7,6},{8,9},{9,8},{10,11... | collective-permute-start | bytes 1179656 | tf_op jit(solution)/shard_map/ppermute | solution.py:31
  233.8 18.6 %collective-permute-start.8 = (bf16[8,96,384]{2,1,0:T(8,128)(2,1)S(1)}, bf16[8,96,384]{2,1,0:T(8,128)(2,1)S(1)}, u32[]{:S(2)}, u32[]{:S(2)}) collective-permute-start(bf16[8,96,384]{2,1,0:T(8,128)(2,1)S(1)} %get-tuple-element.25), channel_id=1, source_target_pairs={{0,1},{1,0},{2,3},{3,2},{4,5},{5,4},{6,7},{7,6},{8,9},{9,8},{10,11... | collective-permute-start | bytes 1769480 | tf_op jit(solution)/shard_map/ppermute | solution.py:31
  (26 other events, 120.7 us)

commit v4 on v3

--- a/solution.py
+++ b/solution.py
@@ -22,9 +22,10 @@
     return lax.ppermute(value, "seg", [(i, i ^ 1) for i in range(count)])
 
 
-def chip_shift(value, step):
+def chip_gather(value):
     count = lax.axis_size("seg")
-    return lax.ppermute(value, "seg", [(i, (i + 2 * step) % count) for i in range(count)])
+    groups = [[i for i in range(count) if i % 2 == core] for core in range(2)]
+    return lax.all_gather(value, "seg", axis_index_groups=groups)
 
 
 def tok_swap(value):
@@ -78,9 +79,7 @@
     given = lax.dynamic_index_in_dim(down_part, 1 - core, 0, keepdims=False)
     pair_sum = kept + core_swap(given)
     pair_sent = pair_sum.astype(BF16)
-    total = pair_sum
-    for step in (1, 2, 3):
-        total = total + chip_shift(pair_sent, step).astype(F32)
+    total = jnp.sum(chip_gather(pair_sent).astype(F32), axis=0)
     mine = shard_gather(total.astype(BF16))
     other = core_swap(mine)
     rows = mine.shape[1]

time: 260 us -> 258 us (level)
  blocking collectives: 69.7 us -> 81.2 us
  starting transfers between devices: 41.4 us -> 34 us
  waiting for transfers between devices: 84.7 us -> 78.2 us
    all_gather x0 -> x1, blocking collectives: none -> 15.4 us  [chip_gather(): return lax.all_gather(value, 'seg', axis_index_groups=groups)]
    ppermute x3 -> x0, starting transfers between devices: 9.34 us -> none  [chip_shift(): lax.ppermute(value, 'seg', [(i, (i + 2 * step) % count) for i in range(co...]
    ppermute x3 -> x0, waiting for transfers between devices: 4.61 us -> none  [chip_shift(): lax.ppermute(value, 'seg', [(i, (i + 2 * step) % count) for i in range(co...]
    all_gather x2, blocking collectives: 37 us -> 33 us  [seg_step(): parts = lax.all_gather(mine, 'seg').astype(F32)]
  transfers between devices with their start and end apart: 17 -> 14, of which waited for: 13 -> 11; matrix products, arithmetic and copies ran while one was open for 14% -> 14% of each run, Pallas kernels for 0% -> 0%
where the time goes in v4:
time: 258 us; the launch traced here: 255 us
  blocking collectives  81.2 us (31%)
  waiting for transfers between devices  78.2 us (30%)
  starting transfers between devices  34 us (13%)
  local copies, waits for them, and re-layouts  22 us (9%)
  matrix products  21.1 us (8%)
  other arithmetic  15.1 us (6%)
  between operations  2.99 us (1%)
    all_to_all x6, waiting for transfers between devices, shard_exchange(): return lax.all_to_all(pieces, 'shard', 0, 0)  58 us
    all_gather x2, blocking collectives, seg_step(): parts = lax.all_gather(mine, 'seg').astype(F32)  33 us
    all_to_all x1, blocking collectives, shard_exchange(): return lax.all_to_all(pieces, 'shard', 0, 0)  32.7 us
    all_to_all x6, starting transfers between devices, shard_exchange(): return lax.all_to_all(pieces, 'shard', 0, 0)  22.6 us
    dot_general x13, matrix products, dot(): lax.dot_general(left, right, (((left_dim,), (right_dim,)), ((), ())), pre...  21.1 us
    ppermute x6, waiting for transfers between devices, tok_swap(): return lax.ppermute(value, 'tok', [(0, 1), (1, 0)])  19.3 us
    all_gather x1, blocking collectives, chip_gather(): return lax.all_gather(value, 'seg', axis_index_groups=groups)  15.4 us
    ppermute x2, starting transfers between devices, core_swap(): return lax.ppermute(value, 'seg', [(i, i ^ 1) for i in range(count)])  6.55 us
  transfers between devices with their start and end apart: 14, of which 11 were waited for; matrix products, arithmetic and copies ran while one was open for 14% of the time, Pallas kernels for 0%

profile of v4, /device:TPU:1, one launch (start us, length us, event | category | flops | bytes accessed | tf_op | source)
XLA Modules:
  0.0 254.7 jit_solution(14069937478550469947)
XLA Ops:
  4.9 32.7 %all_to_all.35 = bf16[16,160,384]{2,1,0:T(8,128)(2,1)S(1)} all-to-all(bf16[16,160,384]{2,1,0:T(8,128)(2,1)S(1)} %pad_maximum_fusion), channel_id=1, replica_groups=mesh['seg'=8,'shard'=16,'tok'=2] {'shard'}, dimensions={0} | all-to-all | bytes 3932160 | tf_op jit(solution)/shard_map/all_to_all | solution.py:36
  39.0 4.3 %all-to-all-start.1 = ((bf16[16,80,384]{2,1,0:T(8,128)(2,1)}), bf16[16,80,384]{2,1,0:T(8,128)(2,1)S(1)}, u32[]{:S(2)}, u32[]{:S(2)}) async-start(bf16[16,80,384]{2,1,0:T(8,128)(2,1)} %broadcast_in_dim.86), calls=%async_computation.1 | async-start | bytes 1966080 | tf_op jit(solution)/shard_map/all_to_all | solution.py:36
  43.3 14.4 %all-to-all-done.1 = bf16[16,80,384]{2,1,0:T(8,128)(2,1)S(1)} async-done(((bf16[16,80,384]{2,1,0:T(8,128)(2,1)}), bf16[16,80,384]{2,1,0:T(8,128)(2,1)S(1)}, u32[]{:S(2)}, u32[]{:S(2)}) %all-to-all-start.1) | async-done | bytes 983072 | tf_op jit(solution)/shard_map/all_to_all | solution.py:36
  58.0 3.1 %collective-permute-start = (f32[80,384]{1,0:T(8,128)S(1)}, f32[80,384]{1,0:T(8,128)S(1)}, u32[]{:S(2)}, u32[]{:S(2)}) collective-permute-start(f32[80,384]{1,0:T(8,128)S(1)} %dynamic-slice_bitcast_fusion), channel_id=1, source_target_pairs={{0,32},{32,0},{64,96},{96,64},{128,160},{160,128},{192,224},{224,1... | collective-permute-start | bytes 368648 | tf_op jit(solution)/shard_map/ppermute | solution.py:22
  62.1 15.4 %all-gather = bf16[320,384]{1,0:T(8,128)(2,1)S(1)} all-gather(bf16[80,384]{1,0:T(8,128)(2,1)S(1)} %fusion.27), channel_id=2, replica_groups={{0,64,128,192},{32,96,160,224},{1,65,129,193},{33,97,161,225},{2,66,130..., dimensions={0}, use_global_device_ids=true | all-gather | bytes 307200 | tf_op jit(solution)/shard_map/all_gather | solution.py:28
  78.6 3.6 %all-to-all-start.2 = ((bf16[16,80,384]{2,1,0:T(8,128)(2,1)}), bf16[16,80,384]{2,1,0:T(8,128)(2,1)S(1)}, u32[]{:S(2)}, u32[]{:S(2)}) async-start(bf16[16,80,384]{2,1,0:T(8,128)(2,1)} %broadcast_in_dim.87), calls=%async_computation.2 | async-start | bytes 1966080 | tf_op jit(solution)/shard_map/all_to_all | solution.py:36
  84.7 11.4 %all-to-all-done.2 = bf16[16,80,384]{2,1,0:T(8,128)(2,1)S(1)} async-done(((bf16[16,80,384]{2,1,0:T(8,128)(2,1)}), bf16[16,80,384]{2,1,0:T(8,128)(2,1)S(1)}, u32[]{:S(2)}, u32[]{:S(2)}) %all-to-all-start.2) | async-done | bytes 983072 | tf_op jit(solution)/shard_map/all_to_all | solution.py:36
  96.1 3.5 %collective-permute-start.1 = (bf16[16,80,384]{2,1,0:T(8,128)(2,1)S(1)}, bf16[16,80,384]{2,1,0:T(8,128)(2,1)S(1)}, u32[]{:S(2)}, u32[]{:S(2)}) collective-permute-start(bf16[16,80,384]{2,1,0:T(8,128)(2,1)S(1)} %all-to-all-done.2), channel_id=1, source_target_pairs={{0,32},{32,0},{64,96},{96,64},{128,160},{160,128},{192,224},{224,1... | collective-permute-start | bytes 2949128 | tf_op jit(solution)/shard_map/ppermute | solution.py:22
  110.4 3.6 %all-to-all-start.4 = ((bf16[16,64,384]{2,1,0:T(8,128)(2,1)}), bf16[16,64,384]{2,1,0:T(8,128)(2,1)S(1)}, u32[]{:S(2)}, u32[]{:S(2)}) async-start(bf16[16,64,384]{2,1,0:T(8,128)(2,1)} %bitcast.82), calls=%async_computation.4 | async-start | bytes 1572864 | tf_op jit(solution)/shard_map/all_to_all | solution.py:36
  118.8 9.3 %all-to-all-done.4 = bf16[16,64,384]{2,1,0:T(8,128)(2,1)S(1)} async-done(((bf16[16,64,384]{2,1,0:T(8,128)(2,1)}), bf16[16,64,384]{2,1,0:T(8,128)(2,1)S(1)}, u32[]{:S(2)}, u32[]{:S(2)}) %all-to-all-start.4) | async-done | bytes 786464 | tf_op jit(solution)/shard_map/all_to_all | solution.py:36
  129.0 3.7 %all-to-all-start.3 = ((bf16[16,96,384]{2,1,0:T(8,128)(2,1)}), bf16[16,96,384]{2,1,0:T(8,128)(2,1)S(1)}, u32[]{:S(2)}, u32[]{:S(2)}) async-start(bf16[16,96,384]{2,1,0:T(8,128)(2,1)} %bitcast.78), calls=%async_computation.3 | async-start | bytes 2359296 | tf_op jit(solution)/shard_map/all_to_all | solution.py:36
  141.4 8.1 %all-to-all-done.3 = bf16[16,96,384]{2,1,0:T(8,128)(2,1)S(1)} async-done(((bf16[16,96,384]{2,1,0:T(8,128)(2,1)}), bf16[16,96,384]{2,1,0:T(8,128)(2,1)S(1)}, u32[]{:S(2)}, u32[]{:S(2)}) %all-to-all-start.3) | async-done | bytes 1179680 | tf_op jit(solution)/shard_map/all_to_all | solution.py:36
  149.7 18.1 %all-gather.1 = bf16[768,384]{1,0:T(8,128)(2,1)S(1)} all-gather(bf16[96,384]{1,0:T(8,128)(2,1)S(1)} %reduce_sum.120), channel_id=3, replica_groups=mesh['seg'=8,'shard'=16,'tok'=2] {'seg'}, dimensions={0}, use_global_device_ids=true | all-gather | bytes 663552 | tf_op jit(solution)/shard_map/all_gather | solution.py:155
  169.1 15.0 %all-gather.2 = bf16[512,384]{1,0:T(8,128)(2,1)S(1)} all-gather(bf16[64,384]{1,0:T(8,128)(2,1)S(1)} %reduce_sum.124), channel_id=4, replica_groups=mesh['seg'=8,'shard'=16,'tok'=2] {'seg'}, dimensions={0}, use_global_device_ids=true | all-gather | bytes 442368 | tf_op jit(solution)/shard_map/all_gather | solution.py:155
  186.4 3.6 %all-to-all-start.6 = ((bf16[16,72,384]{2,1,0:T(8,128)(2,1)}), bf16[16,72,384]{2,1,0:T(8,128)(2,1)S(1)}, u32[]{:S(2)}, u32[]{:S(2)}) async-start(bf16[16,72,384]{2,1,0:T(8,128)(2,1)} %broadcast_in_dim.98), calls=%async_computation.6 | async-start | bytes 1769472 | tf_op jit(solution)/shard_map/all_to_all | solution.py:36
  192.0 13.1 %all-to-all-done.6 = bf16[16,72,384]{2,1,0:T(8,128)(2,1)S(1)} async-done(((bf16[16,72,384]{2,1,0:T(8,128)(2,1)}), bf16[16,72,384]{2,1,0:T(8,128)(2,1)S(1)}, u32[]{:S(2)}, u32[]{:S(2)}) %all-to-all-start.6) | async-done | bytes 884768 | tf_op jit(solution)/shard_map/all_to_all | solution.py:36
  206.3 3.7 %all-to-all-start.5 = ((bf16[16,96,384]{2,1,0:T(8,128)(2,1)}), bf16[16,96,384]{2,1,0:T(8,128)(2,1)S(1)}, u32[]{:S(2)}, u32[]{:S(2)}) async-start(bf16[16,96,384]{2,1,0:T(8,128)(2,1)} %broadcast_in_dim.91), calls=%async_computation.5 | async-start | bytes 2359296 | tf_op jit(solution)/shard_map/all_to_all | solution.py:36
  212.2 2.4 collective-permute-done.2
  220.1 3.0 %collective-permute-done.7 = f32[8,128]{1,0:T(8,128)S(1)} collective-permute-done((f32[8,128]{1,0:T(8,128)S(1)}, f32[8,128]{1,0:T(8,128)S(1)}, u32[]{:S(2)}, u32[]{:S(2)}) %collective-permute-start.7) | collective-permute-done | bytes 4128 | tf_op jit(solution)/shard_map/ppermute | solution.py:32
  226.6 2.5 fusion.35
  233.8 3.7 %collective-permute-done.3 = bf16[512,384]{1,0:T(8,128)(2,1)S(1)} collective-permute-done((bf16[512,384]{1,0:T(8,128)(2,1)S(1)}, bf16[512,384]{1,0:T(8,128)(2,1)S(1)}, u32[]{:S(2)}, u32[]{:S(2)}) %collective-permute-start.3) | collective-permute-done | bytes 393248 | tf_op jit(solution)/shard_map/ppermute | solution.py:32
  237.4 2.4 convolution_add_fusion.1
  239.8 10.2 %collective-permute-done.5 = bf16[8,96,384]{2,1,0:T(8,128)(2,1)S(1)} collective-permute-done((bf16[8,96,384]{2,1,0:T(8,128)(2,1)S(1)}, bf16[8,96,384]{2,1,0:T(8,128)(2,1)S(1)}, u32[]{:S(2)}, u32[]{:S(2)}) %collective-permute-start.5) | collective-permute-done | bytes 589856 | tf_op jit(solution)/shard_map/ppermute | solution.py:32
  250.1 3.5 %convolution_add_fusion = f32[512,1280]{1,0:T(8,128)} fusion(f32[512,1280]{1,0:T(8,128)S(1)} %fusion.6, bf16[512,384]{1,0:T(8,128)(2,1)} %collective-permute-done.4, bf16[512,384]{1,0:T(8,128)(2,1)} %bitcast.30, bf16[768,384]{1,0:T(8,128)(2,1)S(1)} %bitcast.83), kind=kOutput, calls=%fused_computation.1 | convolution fusion | flops 505937920 | bytes 6619136 | tf_op jit(solution)/shard_map/dot_general | solution.py:15
  (136 shorter events, 57.4 us)
Async XLA Ops:
  37.9 19.8 %copy-start.16 = (bf16[1280,160]{0,1:T(8,128)(2,1)S(1)}, bf16[1280,160]{0,1:T(8,128)(2,1)}, u32[]{:S(2)}) copy-start(bf16[1280,160]{0,1:T(8,128)(2,1)} %param.12) | copy-start | bytes 1228804
  39.0 18.6 %all-to-all-start.1 = ((bf16[16,80,384]{2,1,0:T(8,128)(2,1)}), bf16[16,80,384]{2,1,0:T(8,128)(2,1)S(1)}, u32[]{:S(2)}, u32[]{:S(2)}) async-start(bf16[16,80,384]{2,1,0:T(8,128)(2,1)} %broadcast_in_dim.86), calls=%async_computation.1 | async-start | bytes 1966080 | tf_op jit(solution)/shard_map/all_to_all | solution.py:36
  58.0 4.1 %collective-permute-start = (f32[80,384]{1,0:T(8,128)S(1)}, f32[80,384]{1,0:T(8,128)S(1)}, u32[]{:S(2)}, u32[]{:S(2)}) collective-permute-start(f32[80,384]{1,0:T(8,128)S(1)} %dynamic-slice_bitcast_fusion), channel_id=1, source_target_pairs={{0,32},{32,0},{64,96},{96,64},{128,160},{160,128},{192,224},{224,1... | collective-permute-start | bytes 368648 | tf_op jit(solution)/shard_map/ppermute | solution.py:22
  78.6 17.5 %all-to-all-start.2 = ((bf16[16,80,384]{2,1,0:T(8,128)(2,1)}), bf16[16,80,384]{2,1,0:T(8,128)(2,1)S(1)}, u32[]{:S(2)}, u32[]{:S(2)}) async-start(bf16[16,80,384]{2,1,0:T(8,128)(2,1)} %broadcast_in_dim.87), calls=%async_computation.2 | async-start | bytes 1966080 | tf_op jit(solution)/shard_map/all_to_all | solution.py:36
  82.3 17.3 %copy-start.28 = (s32[8]{0:T(128)S(1)}, s32[8]{0:T(128)}, u32[]{:S(2)}) copy-start(s32[8]{0:T(128)} %param.17) | copy-start | bytes 100
  82.3 17.9 %copy-start.20 = (f32[2560]{0:T(1024)S(1)}, f32[2560]{0:T(1024)}, u32[]{:S(2)}) copy-start(f32[2560]{0:T(1024)} %param.16) | copy-start | bytes 30724
  96.1 8.0 %collective-permute-start.1 = (bf16[16,80,384]{2,1,0:T(8,128)(2,1)S(1)}, bf16[16,80,384]{2,1,0:T(8,128)(2,1)S(1)}, u32[]{:S(2)}, u32[]{:S(2)}) collective-permute-start(bf16[16,80,384]{2,1,0:T(8,128)(2,1)S(1)} %all-to-all-done.2), channel_id=1, source_target_pairs={{0,32},{32,0},{64,96},{96,64},{128,160},{160,128},{192,224},{224,1... | collective-permute-start | bytes 2949128 | tf_op jit(solution)/shard_map/ppermute | solution.py:22
  110.4 17.7 %all-to-all-start.4 = ((bf16[16,64,384]{2,1,0:T(8,128)(2,1)}), bf16[16,64,384]{2,1,0:T(8,128)(2,1)S(1)}, u32[]{:S(2)}, u32[]{:S(2)}) async-start(bf16[16,64,384]{2,1,0:T(8,128)(2,1)} %bitcast.82), calls=%async_computation.4 | async-start | bytes 1572864 | tf_op jit(solution)/shard_map/all_to_all | solution.py:36
  129.0 20.5 %all-to-all-start.3 = ((bf16[16,96,384]{2,1,0:T(8,128)(2,1)}), bf16[16,96,384]{2,1,0:T(8,128)(2,1)S(1)}, u32[]{:S(2)}, u32[]{:S(2)}) async-start(bf16[16,96,384]{2,1,0:T(8,128)(2,1)} %bitcast.78), calls=%async_computation.3 | async-start | bytes 2359296 | tf_op jit(solution)/shard_map/all_to_all | solution.py:36
  140.0 27.8 %copy-start.21 = (f32[8]{0:T(128)S(1)}, f32[8]{0:T(128)}, u32[]{:S(2)}) copy-start(f32[8]{0:T(128)} %compare_convert_fusion) | copy-start | bytes 100
  140.0 27.8 %copy-start.22 = (f32[8]{0:T(128)S(1)}, f32[8]{0:T(128)}, u32[]{:S(2)}) copy-start(f32[8]{0:T(128)} %subtract_convert_fusion.2) | copy-start | bytes 100
  141.3 26.8 %copy-start.26 = (f32[96]{0:T(128)S(1)}, f32[96]{0:T(128)}, u32[]{:S(2)}) copy-start(f32[96]{0:T(128)} %dynamic_slice.63) | copy-start | bytes 1156
  141.4 42.9 %copy-start.23 = (f32[64]{0:T(128)S(1)}, f32[64]{0:T(128)}, u32[]{:S(2)}) copy-start(f32[64]{0:T(128)} %dynamic_slice.67) | copy-start | bytes 772
  149.7 35.6 %copy-start.24 = (pred[8]{0:T(512)(128)(4,1)S(1)}, pred[8]{0:T(512)(128)(4,1)}, u32[]{:S(2)}) copy-start(pred[8]{0:T(512)(128)(4,1)} %get-tuple-element.39) | copy-start | bytes 28
  149.7 35.6 %copy-start.25 = (pred[8]{0:T(512)(128)(4,1)S(1)}, pred[8]{0:T(512)(128)(4,1)}, u32[]{:S(2)}) copy-start(pred[8]{0:T(512)(128)(4,1)} %get-tuple-element.40) | copy-start | bytes 28
  186.4 18.7 %all-to-all-start.6 = ((bf16[16,72,384]{2,1,0:T(8,128)(2,1)}), bf16[16,72,384]{2,1,0:T(8,128)(2,1)S(1)}, u32[]{:S(2)}, u32[]{:S(2)}) async-start(bf16[16,72,384]{2,1,0:T(8,128)(2,1)} %broadcast_in_dim.98), calls=%async_computation.6 | async-start | bytes 1769472 | tf_op jit(solution)/shard_map/all_to_all | solution.py:36
  191.1 19.8 %copy-start.9 = (bf16[8,80,384]{2,1,0:T(8,128)(2,1)S(1)}, bf16[8,80,384]{2,1,0:T(8,128)(2,1)}, u32[]{:S(2)}) copy-start(bf16[8,80,384]{2,1,0:T(8,128)(2,1)} %get-tuple-element.30) | copy-start | bytes 1474564
  191.1 23.5 %collective-permute-start.2 = (bf16[16,80,384]{2,1,0:T(8,128)(2,1)}, bf16[16,80,384]{2,1,0:T(8,128)(2,1)}, u32[]{:S(2)}, u32[]{:S(2)}) collective-permute-start(bf16[16,80,384]{2,1,0:T(8,128)(2,1)} %pad_maximum_fusion.3), channel_id=1, source_target_pairs={{0,1},{1,0},{2,3},{3,2},{4,5},{5,4},{6,7},{7,6},{8,9},{9,8},{10,11... | collective-permute-start | bytes 2949128 | tf_op jit(solution)/shard_map/ppermute | solution.py:32
  206.3 20.3 %all-to-all-start.5 = ((bf16[16,96,384]{2,1,0:T(8,128)(2,1)}), bf16[16,96,384]{2,1,0:T(8,128)(2,1)S(1)}, u32[]{:S(2)}, u32[]{:S(2)}) async-start(bf16[16,96,384]{2,1,0:T(8,128)(2,1)} %broadcast_in_dim.91), calls=%async_computation.5 | async-start | bytes 2359296 | tf_op jit(solution)/shard_map/all_to_all | solution.py:36
  210.0 29.8 %collective-permute-start.4 = (bf16[512,384]{1,0:T(8,128)(2,1)}, bf16[512,384]{1,0:T(8,128)(2,1)}, u32[]{:S(2)}, u32[]{:S(2)}) collective-permute-start(bf16[512,384]{1,0:T(8,128)(2,1)} %copy-done.17), channel_id=1, source_target_pairs={{0,1},{1,0},{2,3},{3,2},{4,5},{5,4},{6,7},{7,6},{8,9},{9,8},{10,11... | collective-permute-start | bytes 1179656 | tf_op jit(solution)/shard_map/ppermute | solution.py:32
  217.5 5.6 %collective-permute-start.7 = (f32[8,128]{1,0:T(8,128)S(1)}, f32[8,128]{1,0:T(8,128)S(1)}, u32[]{:S(2)}, u32[]{:S(2)}) collective-permute-start(f32[8,128]{1,0:T(8,128)S(1)} %broadcast_in_dim.99), channel_id=1, source_target_pairs={{0,1},{1,0},{2,3},{3,2},{4,5},{5,4},{6,7},{7,6},{8,9},{9,8},{10,11... | collective-permute-start | bytes 12296 | tf_op jit(solution)/shard_map/ppermute | solution.py:32
  219.5 20.3 %collective-permute-start.6 = (bf16[8,64,384]{2,1,0:T(8,128)(2,1)}, bf16[8,64,384]{2,1,0:T(8,128)(2,1)}, u32[]{:S(2)}, u32[]{:S(2)}) collective-permute-start(bf16[8,64,384]{2,1,0:T(8,128)(2,1)} %get-tuple-element.33), channel_id=1, source_target_pairs={{0,1},{1,0},{2,3},{3,2},{4,5},{5,4},{6,7},{7,6},{8,9},{9,8},{10,11... | collective-permute-start | bytes 1179656 | tf_op jit(solution)/shard_map/ppermute | solution.py:32
  230.0 7.4 %collective-permute-start.3 = (bf16[512,384]{1,0:T(8,128)(2,1)S(1)}, bf16[512,384]{1,0:T(8,128)(2,1)S(1)}, u32[]{:S(2)}, u32[]{:S(2)}) collective-permute-start(bf16[512,384]{1,0:T(8,128)(2,1)S(1)} %fusion.3), channel_id=1, source_target_pairs={{0,1},{1,0},{2,3},{3,2},{4,5},{5,4},{6,7},{7,6},{8,9},{9,8},{10,11... | collective-permute-start | bytes 1179656 | tf_op jit(solution)/shard_map/ppermute | solution.py:32
  231.9 18.1 %collective-permute-start.5 = (bf16[8,96,384]{2,1,0:T(8,128)(2,1)S(1)}, bf16[8,96,384]{2,1,0:T(8,128)(2,1)S(1)}, u32[]{:S(2)}, u32[]{:S(2)}) collective-permute-start(bf16[8,96,384]{2,1,0:T(8,128)(2,1)S(1)} %get-tuple-element.25), channel_id=1, source_target_pairs={{0,1},{1,0},{2,3},{3,2},{4,5},{5,4},{6,7},{7,6},{8,9},{9,8},{10,11... | collective-permute-start | bytes 1769480 | tf_op jit(solution)/shard_map/ppermute | solution.py:32
  (23 other events, 66.3 us)

commit v5 on v3

--- a/solution.py
+++ b/solution.py
@@ -105,8 +105,8 @@
     def tok_half(pieces, which):
         return lax.dynamic_slice_in_dim(pieces, which * (shards // 2), shards // 2, 0)
 
-    sent = [tok_half(c, 1 - tok_index) for c in (centered_mine, centered_other)]
-    centered_peer = tok_swap(jnp.concatenate(sent, axis=0))
+    peer_mine = tok_swap(tok_half(centered_mine, 1 - tok_index))
+    peer_other = tok_swap(tok_half(centered_other, 1 - tok_index))
 
     lat_count = encoder_weight.shape[1]
     size_here = jnp.sum(jnp.where(jnp.arange(segment_total) == segment_index, segment_sizes, 0))
@@ -202,7 +202,7 @@
     grad_decoder = grad_decoder + dot(codes_other, back_other, 1, 1)
     own = by_core(tok_half(centered_mine, tok_index), tok_half(centered_other, tok_index), 1)
     own = lax.optimization_barrier(own.reshape(half, tokens))
-    peer = by_core(centered_peer[:count], centered_peer[count:], 1)
+    peer = by_core(peer_mine, peer_other, 1)
     peer = lax.optimization_barrier(peer.reshape(half, tokens))
     grad_encoder = dot(own, code_grad, 1, 1)
     grad_encoder = grad_encoder + dot(peer, code_grad_other, 1, 1)

time: 260 us -> 269 us (1.035)
  waiting for transfers between devices: 84.7 us -> 89.9 us
  local copies, waits for them, and re-layouts: 22 us -> 18.8 us
  matrix products: 21.1 us -> 24.2 us
    ppermute x6 -> x7, waiting for transfers between devices: 20.4 us -> 28.2 us  [tok_swap(): return lax.ppermute(value, 'tok', [(0, 1), (1, 0)])]
    dot_general x13, matrix products: 21.1 us -> 24.2 us  [dot(): lax.dot_general(left, right, (((left_dim,), (right_dim,)), ((), ())), pre...]
    select_n x3, other arithmetic: 3.41 us -> 6.11 us  [by_core(): jnp.where(core == 0, jnp.concatenate([here, there], axis=dim), jnp.concat...]
  transfers between devices with their start and end apart: 17 -> 18, of which waited for: 13 -> 12; matrix products, arithmetic and copies ran while one was open for 14% -> 14% of each run, Pallas kernels for 0% -> 0%
where the time goes in v5:
time: 269 us; the launch traced here: 266 us
  waiting for transfers between devices  89.9 us (33%)
  blocking collectives  69.6 us (26%)
  starting transfers between devices  43.1 us (16%)
  matrix products  24.2 us (9%)
  local copies, waits for them, and re-layouts  18.8 us (7%)
  other arithmetic  17.4 us (6%)
  between operations  2.96 us (1%)
    all_to_all x6, waiting for transfers between devices, shard_exchange(): return lax.all_to_all(pieces, 'shard', 0, 0)  56.1 us
    all_gather x2, blocking collectives, seg_step(): parts = lax.all_gather(mine, 'seg').astype(F32)  36.9 us
    all_to_all x1, blocking collectives, shard_exchange(): return lax.all_to_all(pieces, 'shard', 0, 0)  32.7 us
    ppermute x7, waiting for transfers between devices, tok_swap(): return lax.ppermute(value, 'tok', [(0, 1), (1, 0)])  28.2 us
    dot_general x13, matrix products, dot(): lax.dot_general(left, right, (((left_dim,), (right_dim,)), ((), ())), pre...  24.2 us
    all_to_all x6, starting transfers between devices, shard_exchange(): return lax.all_to_all(pieces, 'shard', 0, 0)  22.7 us
    ppermute x3, starting transfers between devices, chip_shift(): lax.ppermute(value, 'seg', [(i, (i + 2 * step) % count) for i in range(co...  9.34 us
    ppermute x2, starting transfers between devices, core_swap(): return lax.ppermute(value, 'seg', [(i, i ^ 1) for i in range(count)])  6.3 us
  transfers between devices with their start and end apart: 18, of which 12 were waited for; matrix products, arithmetic and copies ran while one was open for 14% of the time, Pallas kernels for 0%

profile of v5, /device:TPU:1, one launch (start us, length us, event | category | flops | bytes accessed | tf_op | source)
XLA Modules:
  0.0 265.9 jit_solution(2605097600540134473)
XLA Ops:
  4.9 32.7 %all_to_all.35 = bf16[16,160,384]{2,1,0:T(8,128)(2,1)S(1)} all-to-all(bf16[16,160,384]{2,1,0:T(8,128)(2,1)S(1)} %pad_maximum_fusion), channel_id=1, replica_groups=mesh['seg'=8,'shard'=16,'tok'=2] {'shard'}, dimensions={0} | all-to-all | bytes 3932160 | tf_op jit(solution)/shard_map/all_to_all | solution.py:35
  39.0 4.3 %all-to-all-start.1 = ((bf16[16,80,384]{2,1,0:T(8,128)(2,1)}), bf16[16,80,384]{2,1,0:T(8,128)(2,1)S(1)}, u32[]{:S(2)}, u32[]{:S(2)}) async-start(bf16[16,80,384]{2,1,0:T(8,128)(2,1)} %broadcast_in_dim.86), calls=%async_computation.1 | async-start | bytes 1966080 | tf_op jit(solution)/shard_map/all_to_all | solution.py:35
  43.3 14.4 %all-to-all-done.1 = bf16[16,80,384]{2,1,0:T(8,128)(2,1)S(1)} async-done(((bf16[16,80,384]{2,1,0:T(8,128)(2,1)}), bf16[16,80,384]{2,1,0:T(8,128)(2,1)S(1)}, u32[]{:S(2)}, u32[]{:S(2)}) %all-to-all-start.1) | async-done | bytes 983072 | tf_op jit(solution)/shard_map/all_to_all | solution.py:35
  58.0 3.1 %collective-permute-start = (f32[80,384]{1,0:T(8,128)S(1)}, f32[80,384]{1,0:T(8,128)S(1)}, u32[]{:S(2)}, u32[]{:S(2)}) collective-permute-start(f32[80,384]{1,0:T(8,128)S(1)} %dynamic-slice_bitcast_fusion), channel_id=1, source_target_pairs={{0,32},{32,0},{64,96},{96,64},{128,160},{160,128},{192,224},{224,1... | collective-permute-start | bytes 368648 | tf_op jit(solution)/shard_map/ppermute | solution.py:22
  62.1 6.1 %collective-permute-start.3 = (bf16[80,384]{1,0:T(8,128)(2,1)S(1)}, bf16[80,384]{1,0:T(8,128)(2,1)S(1)}, u32[]{:S(2)}, u32[]{:S(2)}) collective-permute-start(bf16[80,384]{1,0:T(8,128)(2,1)S(1)} %fusion.27), channel_id=1, source_target_pairs={{0,192},{32,224},{64,0},{96,32},{128,64},{160,96},{192,128},{224,1... | collective-permute-start | bytes 184328 | tf_op jit(solution)/shard_map/ppermute | solution.py:27
  71.5 3.9 %collective-permute-done.2 = bf16[80,384]{1,0:T(8,128)(2,1)S(1)} collective-permute-done((bf16[80,384]{1,0:T(8,128)(2,1)S(1)}, bf16[80,384]{1,0:T(8,128)(2,1)S(1)}, u32[]{:S(2)}, u32[]{:S(2)}) %collective-permute-start.2) | collective-permute-done | bytes 61472 | tf_op jit(solution)/shard_map/ppermute | solution.py:27
  77.1 3.6 %all-to-all-start.2 = ((bf16[16,80,384]{2,1,0:T(8,128)(2,1)}), bf16[16,80,384]{2,1,0:T(8,128)(2,1)S(1)}, u32[]{:S(2)}, u32[]{:S(2)}) async-start(bf16[16,80,384]{2,1,0:T(8,128)(2,1)} %broadcast_in_dim.87), calls=%async_computation.2 | async-start | bytes 1966080 | tf_op jit(solution)/shard_map/all_to_all | solution.py:35
  83.2 11.7 %all-to-all-done.2 = bf16[16,80,384]{2,1,0:T(8,128)(2,1)S(1)} async-done(((bf16[16,80,384]{2,1,0:T(8,128)(2,1)}), bf16[16,80,384]{2,1,0:T(8,128)(2,1)S(1)}, u32[]{:S(2)}, u32[]{:S(2)}) %all-to-all-start.2) | async-done | bytes 983072 | tf_op jit(solution)/shard_map/all_to_all | solution.py:35
  94.9 3.2 %collective-permute-start.4 = (bf16[16,80,384]{2,1,0:T(8,128)(2,1)S(1)}, bf16[16,80,384]{2,1,0:T(8,128)(2,1)S(1)}, u32[]{:S(2)}, u32[]{:S(2)}) collective-permute-start(bf16[16,80,384]{2,1,0:T(8,128)(2,1)S(1)} %all-to-all-done.2), channel_id=1, source_target_pairs={{0,32},{32,0},{64,96},{96,64},{128,160},{160,128},{192,224},{224,1... | collective-permute-start | bytes 2949128 | tf_op jit(solution)/shard_map/ppermute | solution.py:22
  108.3 3.6 %all-to-all-start.4 = ((bf16[16,64,384]{2,1,0:T(8,128)(2,1)}), bf16[16,64,384]{2,1,0:T(8,128)(2,1)S(1)}, u32[]{:S(2)}, u32[]{:S(2)}) async-start(bf16[16,64,384]{2,1,0:T(8,128)(2,1)} %bitcast.83), calls=%async_computation.4 | async-start | bytes 1572864 | tf_op jit(solution)/shard_map/all_to_all | solution.py:35
  117.7 8.3 %all-to-all-done.4 = bf16[16,64,384]{2,1,0:T(8,128)(2,1)S(1)} async-done(((bf16[16,64,384]{2,1,0:T(8,128)(2,1)}), bf16[16,64,384]{2,1,0:T(8,128)(2,1)S(1)}, u32[]{:S(2)}, u32[]{:S(2)}) %all-to-all-start.4) | async-done | bytes 786464 | tf_op jit(solution)/shard_map/all_to_all | solution.py:35
  126.9 3.9 %all-to-all-start.3 = ((bf16[16,96,384]{2,1,0:T(8,128)(2,1)}), bf16[16,96,384]{2,1,0:T(8,128)(2,1)S(1)}, u32[]{:S(2)}, u32[]{:S(2)}) async-start(bf16[16,96,384]{2,1,0:T(8,128)(2,1)} %bitcast.82), calls=%async_computation.3 | async-start | bytes 2359296 | tf_op jit(solution)/shard_map/all_to_all | solution.py:35
  135.1 3.2 %maximum_select_fusion = bf16[16,160,384]{2,1,0:T(8,128)(2,1)} fusion(bf16[16,80,384]{2,1,0:T(8,128)(2,1)} %copy-done.4, bf16[16,80,384]{2,1,0:T(8,128)(2,1)S(1)} %all-to-all-done.2, pred[]{:T(512)S(6)} %eq.27), kind=kLoop, calls=%fused_computation.8 | loop fusion | flops 8847360 | bytes 3932161 | tf_op jit(solution)/shard_map/jit(_where)/select_n | solution.py:89
  139.6 7.8 %all-to-all-done.3 = bf16[16,96,384]{2,1,0:T(8,128)(2,1)S(1)} async-done(((bf16[16,96,384]{2,1,0:T(8,128)(2,1)}), bf16[16,96,384]{2,1,0:T(8,128)(2,1)S(1)}, u32[]{:S(2)}, u32[]{:S(2)}) %all-to-all-start.3) | async-done | bytes 1179680 | tf_op jit(solution)/shard_map/all_to_all | solution.py:35
  147.6 21.9 %all-gather = bf16[768,384]{1,0:T(8,128)(2,1)S(1)} all-gather(bf16[96,384]{1,0:T(8,128)(2,1)S(1)} %reduce_sum.107), channel_id=2, replica_groups=mesh['seg'=8,'shard'=16,'tok'=2] {'seg'}, dimensions={0}, use_global_device_ids=true | all-gather | bytes 663552 | tf_op jit(solution)/shard_map/all_gather | solution.py:156
  170.8 15.0 %all-gather.1 = bf16[512,384]{1,0:T(8,128)(2,1)S(1)} all-gather(bf16[64,384]{1,0:T(8,128)(2,1)S(1)} %reduce_sum.111), channel_id=3, replica_groups=mesh['seg'=8,'shard'=16,'tok'=2] {'seg'}, dimensions={0}, use_global_device_ids=true | all-gather | bytes 442368 | tf_op jit(solution)/shard_map/all_gather | solution.py:156
  188.9 3.6 %all-to-all-start.6 = ((bf16[16,72,384]{2,1,0:T(8,128)(2,1)}), bf16[16,72,384]{2,1,0:T(8,128)(2,1)S(1)}, u32[]{:S(2)}, u32[]{:S(2)}) async-start(bf16[16,72,384]{2,1,0:T(8,128)(2,1)} %broadcast_in_dim.98), calls=%async_computation.6 | async-start | bytes 1769472 | tf_op jit(solution)/shard_map/all_to_all | solution.py:35
  193.6 14.0 %all-to-all-done.6 = bf16[16,72,384]{2,1,0:T(8,128)(2,1)S(1)} async-done(((bf16[16,72,384]{2,1,0:T(8,128)(2,1)}), bf16[16,72,384]{2,1,0:T(8,128)(2,1)S(1)}, u32[]{:S(2)}, u32[]{:S(2)}) %all-to-all-start.6) | async-done | bytes 884768 | tf_op jit(solution)/shard_map/all_to_all | solution.py:35
  208.8 3.7 %all-to-all-start.5 = ((bf16[16,96,384]{2,1,0:T(8,128)(2,1)}), bf16[16,96,384]{2,1,0:T(8,128)(2,1)S(1)}, u32[]{:S(2)}, u32[]{:S(2)}) async-start(bf16[16,96,384]{2,1,0:T(8,128)(2,1)} %broadcast_in_dim.91), calls=%async_computation.5 | async-start | bytes 2359296 | tf_op jit(solution)/shard_map/all_to_all | solution.py:35
  215.5 8.3 %collective-permute-done.6 = bf16[8,80,384]{2,1,0:T(8,128)(2,1)S(1)} collective-permute-done((bf16[8,80,384]{2,1,0:T(8,128)(2,1)S(1)}, bf16[8,80,384]{2,1,0:T(8,128)(2,1)S(1)}, u32[]{:S(2)}, u32[]{:S(2)}) %collective-permute-start.6) | collective-permute-done | bytes 491552 | tf_op jit(solution)/shard_map/ppermute | solution.py:31
  229.2 3.2 %collective-permute-done.11 = f32[8,128]{1,0:T(8,128)S(1)} collective-permute-done((f32[8,128]{1,0:T(8,128)S(1)}, f32[8,128]{1,0:T(8,128)S(1)}, u32[]{:S(2)}, u32[]{:S(2)}) %collective-permute-start.11) | collective-permute-done | bytes 4128 | tf_op jit(solution)/shard_map/ppermute | solution.py:31
  242.2 6.5 %collective-permute-done.7 = bf16[512,384]{1,0:T(8,128)(2,1)S(1)} collective-permute-done((bf16[512,384]{1,0:T(8,128)(2,1)S(1)}, bf16[512,384]{1,0:T(8,128)(2,1)S(1)}, u32[]{:S(2)}, u32[]{:S(2)}) %collective-permute-start.7) | collective-permute-done | bytes 393248 | tf_op jit(solution)/shard_map/ppermute | solution.py:31
  251.1 10.2 %collective-permute-done.9 = bf16[8,96,384]{2,1,0:T(8,128)(2,1)S(1)} collective-permute-done((bf16[8,96,384]{2,1,0:T(8,128)(2,1)S(1)}, bf16[8,96,384]{2,1,0:T(8,128)(2,1)S(1)}, u32[]{:S(2)}, u32[]{:S(2)}) %collective-permute-start.9) | collective-permute-done | bytes 589856 | tf_op jit(solution)/shard_map/ppermute | solution.py:31
  261.3 3.5 %convolution_add_fusion = f32[512,1280]{1,0:T(8,128)} fusion(f32[512,1280]{1,0:T(8,128)S(1)} %fusion.6, bf16[512,384]{1,0:T(8,128)(2,1)} %collective-permute-done.8, bf16[512,384]{1,0:T(8,128)(2,1)} %bitcast.29, bf16[768,384]{1,0:T(8,128)(2,1)S(1)} %bitcast.84), kind=kOutput, calls=%fused_computation.1 | convolution fusion | flops 505937920 | bytes 6619136 | tf_op jit(solution)/shard_map/dot_general | solution.py:15
  (125 shorter events, 63.3 us)
Async XLA Ops:
  39.0 18.6 %all-to-all-start.1 = ((bf16[16,80,384]{2,1,0:T(8,128)(2,1)}), bf16[16,80,384]{2,1,0:T(8,128)(2,1)S(1)}, u32[]{:S(2)}, u32[]{:S(2)}) async-start(bf16[16,80,384]{2,1,0:T(8,128)(2,1)} %broadcast_in_dim.86), calls=%async_computation.1 | async-start | bytes 1966080 | tf_op jit(solution)/shard_map/all_to_all | solution.py:35
  58.0 4.1 %collective-permute-start = (f32[80,384]{1,0:T(8,128)S(1)}, f32[80,384]{1,0:T(8,128)S(1)}, u32[]{:S(2)}, u32[]{:S(2)}) collective-permute-start(f32[80,384]{1,0:T(8,128)S(1)} %dynamic-slice_bitcast_fusion), channel_id=1, source_target_pairs={{0,32},{32,0},{64,96},{96,64},{128,160},{160,128},{192,224},{224,1... | collective-permute-start | bytes 368648 | tf_op jit(solution)/shard_map/ppermute | solution.py:22
  62.1 9.3 %collective-permute-start.3 = (bf16[80,384]{1,0:T(8,128)(2,1)S(1)}, bf16[80,384]{1,0:T(8,128)(2,1)S(1)}, u32[]{:S(2)}, u32[]{:S(2)}) collective-permute-start(bf16[80,384]{1,0:T(8,128)(2,1)S(1)} %fusion.27), channel_id=1, source_target_pairs={{0,192},{32,224},{64,0},{96,32},{128,64},{160,96},{192,128},{224,1... | collective-permute-start | bytes 184328 | tf_op jit(solution)/shard_map/ppermute | solution.py:27
  68.2 7.2 %collective-permute-start.2 = (bf16[80,384]{1,0:T(8,128)(2,1)S(1)}, bf16[80,384]{1,0:T(8,128)(2,1)S(1)}, u32[]{:S(2)}, u32[]{:S(2)}) collective-permute-start(bf16[80,384]{1,0:T(8,128)(2,1)S(1)} %fusion.27), channel_id=1, source_target_pairs={{0,128},{32,160},{64,192},{96,224},{128,0},{160,32},{192,64},{224,... | collective-permute-start | bytes 184328 | tf_op jit(solution)/shard_map/ppermute | solution.py:27
  69.2 6.9 %collective-permute-start.1 = (bf16[80,384]{1,0:T(8,128)(2,1)S(1)}, bf16[80,384]{1,0:T(8,128)(2,1)S(1)}, u32[]{:S(2)}, u32[]{:S(2)}) collective-permute-start(bf16[80,384]{1,0:T(8,128)(2,1)S(1)} %fusion.27), channel_id=1, source_target_pairs={{0,64},{32,96},{64,128},{96,160},{128,192},{160,224},{192,0},{224,... | collective-permute-start | bytes 184328 | tf_op jit(solution)/shard_map/ppermute | solution.py:27
  77.1 17.8 %all-to-all-start.2 = ((bf16[16,80,384]{2,1,0:T(8,128)(2,1)}), bf16[16,80,384]{2,1,0:T(8,128)(2,1)S(1)}, u32[]{:S(2)}, u32[]{:S(2)}) async-start(bf16[16,80,384]{2,1,0:T(8,128)(2,1)} %broadcast_in_dim.87), calls=%async_computation.2 | async-start | bytes 1966080 | tf_op jit(solution)/shard_map/all_to_all | solution.py:35
  94.9 7.8 %collective-permute-start.4 = (bf16[16,80,384]{2,1,0:T(8,128)(2,1)S(1)}, bf16[16,80,384]{2,1,0:T(8,128)(2,1)S(1)}, u32[]{:S(2)}, u32[]{:S(2)}) collective-permute-start(bf16[16,80,384]{2,1,0:T(8,128)(2,1)S(1)} %all-to-all-done.2), channel_id=1, source_target_pairs={{0,32},{32,0},{64,96},{96,64},{128,160},{160,128},{192,224},{224,1... | collective-permute-start | bytes 2949128 | tf_op jit(solution)/shard_map/ppermute | solution.py:22
  108.3 17.7 %all-to-all-start.4 = ((bf16[16,64,384]{2,1,0:T(8,128)(2,1)}), bf16[16,64,384]{2,1,0:T(8,128)(2,1)S(1)}, u32[]{:S(2)}, u32[]{:S(2)}) async-start(bf16[16,64,384]{2,1,0:T(8,128)(2,1)} %bitcast.83), calls=%async_computation.4 | async-start | bytes 1572864 | tf_op jit(solution)/shard_map/all_to_all | solution.py:35
  126.9 20.5 %all-to-all-start.3 = ((bf16[16,96,384]{2,1,0:T(8,128)(2,1)}), bf16[16,96,384]{2,1,0:T(8,128)(2,1)S(1)}, u32[]{:S(2)}, u32[]{:S(2)}) async-start(bf16[16,96,384]{2,1,0:T(8,128)(2,1)} %bitcast.82), calls=%async_computation.3 | async-start | bytes 2359296 | tf_op jit(solution)/shard_map/all_to_all | solution.py:35
  138.4 31.1 %copy-start.14 = (f32[8]{0:T(128)S(1)}, f32[8]{0:T(128)}, u32[]{:S(2)}) copy-start(f32[8]{0:T(128)} %compare_convert_fusion) | copy-start | bytes 100
  138.4 31.1 %copy-start.15 = (f32[8]{0:T(128)S(1)}, f32[8]{0:T(128)}, u32[]{:S(2)}) copy-start(f32[8]{0:T(128)} %subtract_convert_fusion.2) | copy-start | bytes 100
  138.4 31.4 %copy-start.18 = (f32[96]{0:T(128)S(1)}, f32[96]{0:T(128)}, u32[]{:S(2)}) copy-start(f32[96]{0:T(128)} %dynamic_slice.63) | copy-start | bytes 1156
  147.6 40.2 %copy-start.16 = (pred[8]{0:T(512)(128)(4,1)S(1)}, pred[8]{0:T(512)(128)(4,1)}, u32[]{:S(2)}) copy-start(pred[8]{0:T(512)(128)(4,1)} %get-tuple-element.37) | copy-start | bytes 28
  147.6 40.2 %copy-start.17 = (pred[8]{0:T(512)(128)(4,1)S(1)}, pred[8]{0:T(512)(128)(4,1)}, u32[]{:S(2)}) copy-start(pred[8]{0:T(512)(128)(4,1)} %get-tuple-element.38) | copy-start | bytes 28
  188.9 18.7 %all-to-all-start.6 = ((bf16[16,72,384]{2,1,0:T(8,128)(2,1)}), bf16[16,72,384]{2,1,0:T(8,128)(2,1)S(1)}, u32[]{:S(2)}, u32[]{:S(2)}) async-start(bf16[16,72,384]{2,1,0:T(8,128)(2,1)} %broadcast_in_dim.98), calls=%async_computation.6 | async-start | bytes 1769472 | tf_op jit(solution)/shard_map/all_to_all | solution.py:35
  193.6 21.9 %collective-permute-start.5 = (bf16[8,80,384]{2,1,0:T(8,128)(2,1)}, bf16[8,80,384]{2,1,0:T(8,128)(2,1)}, u32[]{:S(2)}, u32[]{:S(2)}) collective-permute-start(bf16[8,80,384]{2,1,0:T(8,128)(2,1)} %get-tuple-element.27), channel_id=1, source_target_pairs={{0,1},{1,0},{2,3},{3,2},{4,5},{5,4},{6,7},{7,6},{8,9},{9,8},{10,11... | collective-permute-start | bytes 1474568 | tf_op jit(solution)/shard_map/ppermute | solution.py:31
  207.6 21.6 %copy-start.1 = (bf16[16,72,384]{2,1,0:T(8,128)(2,1)}, bf16[16,72,384]{2,1,0:T(8,128)(2,1)S(1)}, u32[]{:S(2)}) copy-start(bf16[16,72,384]{2,1,0:T(8,128)(2,1)S(1)} %all-to-all-done.6) | copy-start | bytes 2654212
  208.8 25.4 %all-to-all-start.5 = ((bf16[16,96,384]{2,1,0:T(8,128)(2,1)}), bf16[16,96,384]{2,1,0:T(8,128)(2,1)S(1)}, u32[]{:S(2)}, u32[]{:S(2)}) async-start(bf16[16,96,384]{2,1,0:T(8,128)(2,1)} %broadcast_in_dim.91), calls=%async_computation.5 | async-start | bytes 2359296 | tf_op jit(solution)/shard_map/all_to_all | solution.py:35
  212.6 11.2 %collective-permute-start.6 = (bf16[8,80,384]{2,1,0:T(8,128)(2,1)S(1)}, bf16[8,80,384]{2,1,0:T(8,128)(2,1)S(1)}, u32[]{:S(2)}, u32[]{:S(2)}) collective-permute-start(bf16[8,80,384]{2,1,0:T(8,128)(2,1)S(1)} %get-tuple-element.29), channel_id=1, source_target_pairs={{0,1},{1,0},{2,3},{3,2},{4,5},{5,4},{6,7},{7,6},{8,9},{9,8},{10,11... | collective-permute-start | bytes 1474568 | tf_op jit(solution)/shard_map/ppermute | solution.py:31
  212.7 38.4 %collective-permute-start.8 = (bf16[512,384]{1,0:T(8,128)(2,1)}, bf16[512,384]{1,0:T(8,128)(2,1)}, u32[]{:S(2)}, u32[]{:S(2)}) collective-permute-start(bf16[512,384]{1,0:T(8,128)(2,1)} %get-tuple-element.35), channel_id=1, source_target_pairs={{0,1},{1,0},{2,3},{3,2},{4,5},{5,4},{6,7},{7,6},{8,9},{9,8},{10,11... | collective-permute-start | bytes 1179656 | tf_op jit(solution)/shard_map/ppermute | solution.py:31
  226.6 5.8 %collective-permute-start.11 = (f32[8,128]{1,0:T(8,128)S(1)}, f32[8,128]{1,0:T(8,128)S(1)}, u32[]{:S(2)}, u32[]{:S(2)}) collective-permute-start(f32[8,128]{1,0:T(8,128)S(1)} %broadcast_in_dim.99), channel_id=1, source_target_pairs={{0,1},{1,0},{2,3},{3,2},{4,5},{5,4},{6,7},{7,6},{8,9},{9,8},{10,11... | collective-permute-start | bytes 12296 | tf_op jit(solution)/shard_map/ppermute | solution.py:31
  228.0 23.1 %collective-permute-start.10 = (bf16[8,64,384]{2,1,0:T(8,128)(2,1)}, bf16[8,64,384]{2,1,0:T(8,128)(2,1)}, u32[]{:S(2)}, u32[]{:S(2)}) collective-permute-start(bf16[8,64,384]{2,1,0:T(8,128)(2,1)} %get-tuple-element.31), channel_id=1, source_target_pairs={{0,1},{1,0},{2,3},{3,2},{4,5},{5,4},{6,7},{7,6},{8,9},{9,8},{10,11... | collective-permute-start | bytes 1179656 | tf_op jit(solution)/shard_map/ppermute | solution.py:31
  237.6 11.0 %collective-permute-start.7 = (bf16[512,384]{1,0:T(8,128)(2,1)S(1)}, bf16[512,384]{1,0:T(8,128)(2,1)S(1)}, u32[]{:S(2)}, u32[]{:S(2)}) collective-permute-start(bf16[512,384]{1,0:T(8,128)(2,1)S(1)} %fusion.3), channel_id=1, source_target_pairs={{0,1},{1,0},{2,3},{3,2},{4,5},{5,4},{6,7},{7,6},{8,9},{9,8},{10,11... | collective-permute-start | bytes 1179656 | tf_op jit(solution)/shard_map/ppermute | solution.py:31
  239.1 22.2 %collective-permute-start.9 = (bf16[8,96,384]{2,1,0:T(8,128)(2,1)S(1)}, bf16[8,96,384]{2,1,0:T(8,128)(2,1)S(1)}, u32[]{:S(2)}, u32[]{:S(2)}) collective-permute-start(bf16[8,96,384]{2,1,0:T(8,128)(2,1)S(1)} %get-tuple-element.25), channel_id=1, source_target_pairs={{0,1},{1,0},{2,3},{3,2},{4,5},{5,4},{6,7},{7,6},{8,9},{9,8},{10,11... | collective-permute-start | bytes 1769480 | tf_op jit(solution)/shard_map/ppermute | solution.py:31
  (19 other events, 89.8 us)
